TPU v7x, 512 devices: a whole 4x8x8 slice. The times are simulated.
512 devices in a mesh: view: 64 (over y, z), chord: 8 (over x, core).
Axes of the slice: x: 4, y: 8, z: 8, core: 2. Of those that a mesh axis runs over, the one named last changes fastest.
Arguments:
- proj: bfloat16 [768, 4096, 128], P('view', 'chord'), may hold values from -16 to 16
- tiles: bfloat16 [384, 256, 1024], P('view'), may hold values from -0.01953125 to 0.01953125
- owner: int32 [8, 512], replicated, may hold values from 0 to 511, as said below
- lengths: int32 [8, 512], replicated, may hold values from 1 to 1024, as said below
Outputs:
- recon: float32 [8, 512, 1024], P('chord', 'view')
Inputs may be any that keep to these rules, and one draw needn't show every extreme that they name: `owner`: each row is an ordering of the 512 chords of one group. In each group, the lengths of the chords at owner positions k * 8 to k * 8 + 7 sum to at most 4608, exactly 4608 for some k; the largest entry of each row is 1024.
All inputs are finite; a program needn't handle non-finite values.
Results may differ from a plain program's by a relative error of at most 0.0003.
Values sent between devices are 32-bit elements; how exact they have to be, the bound alone decides.
A program may use at most 64 MiB of HBM per device.

v0:
```python
import functools
import math

import jax
import jax.numpy as jnp
from jax import lax
from jax.experimental import pallas as pl
from jax.experimental.pallas import tpu as pltpu
from jax.sharding import PartitionSpec as P

LANES = 128
PACK = 4608
MESH = pl.DeviceIdType.MESH


def kernel_table(rows, start, cols):
    row_pos = start + jnp.arange(rows, dtype=jnp.float32)[:, None]
    col_pos = jnp.arange(cols, dtype=jnp.float32)[None, :]
    return 1.0 / (row_pos - col_pos + 0.5)


def weigh(length, count, start):
    position = start + jnp.arange(count, dtype=jnp.float32)[None, :] + 0.5
    inside = position < length
    return (inside, jnp.sqrt(jnp.where(inside, position * (length - position), 1.0)))


def invert_block(sums, length, table, start):
    length = length.astype(jnp.float32)[:, None]
    col_in, col_w = weigh(length, sums.shape[1], 0.0)
    row_in, row_w = weigh(length, table.shape[0], start)
    scaled = jnp.where(col_in, col_w * sums, 0.0)
    image = jnp.dot(
        scaled, table.T, precision=lax.Precision.HIGH, preferred_element_type=jnp.float32
    )
    return jnp.where(row_in, image / (math.pi * row_w), 0.0)


def pick(table, index):
    hit = index[:, :, None] == jnp.arange(table.shape[1], dtype=jnp.int32)
    return jnp.sum(jnp.where(hit, table[:, None, :], 0), axis=-1)


def run_rings(rings):
    copies_at = []
    for s in range(max(r["n"] // 2 for r in rings)):
        copies = []
        for r in rings:
            n = r["n"]
            nr = n // 2
            nl = n - 1 - nr
            for go, steps, to, recv, send, sem in (
                (1, nr, r["right"], r["rr"], r["sr"], r["base"] + s),
                (-1, nl, r["left"], r["rl"], r["sl"], r["base"] + nr + s),
            ):
                if s >= steps:
                    continue
                dest = lax.rem(r["me"] + go * (steps - s) + 2 * n, n)
                if s == 0:
                    src = r["chunk"].at[dest]
                else:
                    send[s] = recv[s - 1] + r["chunk"][dest]
                    src = send.at[s]
                copy = pltpu.make_async_remote_copy(
                    src_ref=src,
                    dst_ref=recv.at[s],
                    send_sem=r["ssem"].at[sem],
                    recv_sem=r["rsem"].at[sem],
                    device_id=to,
                    device_id_type=MESH,
                )
                copy.start()
                copies.append(copy)
        for copy in copies:
            copy.wait()
    return [(r["rr"].at[r["n"] // 2 - 1], r["rl"].at[r["n"] - 2 - r["n"] // 2]) for r in rings]


def rs_kernel(ny, nz, xa, xb, oa, ob, s1a, s1b, *bufs):
    ssem, rsem = bufs[-2:]
    bufs = bufs[:-2]
    view = lax.axis_index("view")
    group = lax.axis_index("chord")
    y = view // nz
    z = lax.rem(view, nz)

    def dev(yy, zz):
        return (yy * nz + zz, group)

    z_right = dev(y, lax.rem(z + 1, nz))
    z_left = dev(y, lax.rem(z + nz - 1, nz))
    y_right = dev(lax.rem(y + 1, ny), z)
    y_left = dev(lax.rem(y + ny - 1, ny), z)

    barrier = pltpu.get_barrier_semaphore()
    for peer in (z_right, z_left, y_right, y_left):
        pl.semaphore_signal(barrier, inc=1, device_id=peer, device_id_type=MESH)
    pl.semaphore_wait(barrier, 4)

    def ring(n, me, right, left, chunk, at, base):
        rr, rl, sr, sl = bufs[4 * at: 4 * at + 4]
        return dict(n=n, me=me, right=right, left=left, chunk=chunk, rr=rr, rl=rl, sr=sr, sl=sl,
                    ssem=ssem, rsem=rsem, base=base)

    (ar, al), (br, bl) = run_rings([
        ring(nz, z, z_right, z_left, xa, 0, 0),
        ring(ny, y, y_right, y_left, xb, 1, nz - 1),
    ])
    s1a[...] = xa[z] + ar[...] + al[...]
    s1b[...] = xb[y] + br[...] + bl[...]
    (ar, al), (br, bl) = run_rings([
        ring(ny, y, y_right, y_left, s1a, 2, nz + ny - 2),
        ring(nz, z, z_right, z_left, s1b, 3, nz + 2 * ny - 3),
    ])
    oa[...] = s1a[y] + ar[...] + al[...]
    ob[...] = s1b[z] + br[...] + bl[...]


def reduce_scatter(xa, xb, ny, nz):
    ra, rb = xa.shape[2], xb.shape[2]
    f32 = jnp.float32

    def slots(n, shape):
        return [pltpu.VMEM((n // 2,) + shape, f32), pltpu.VMEM((n - 1 - n // 2,) + shape, f32)] * 2

    bufs = (
        slots(nz, (ny, ra, LANES)) + slots(ny, (nz, rb, LANES))
        + slots(ny, (ra, LANES)) + slots(nz, (rb, LANES))
    )
    return pl.pallas_call(
        functools.partial(rs_kernel, ny, nz),
        out_shape=(jax.ShapeDtypeStruct((ra, LANES), f32), jax.ShapeDtypeStruct((rb, LANES), f32)),
        in_specs=[pl.BlockSpec(memory_space=pltpu.VMEM)] * 2,
        out_specs=(pl.BlockSpec(memory_space=pltpu.VMEM),) * 2,
        scratch_shapes=[pltpu.VMEM((ny, ra, LANES), f32), pltpu.VMEM((nz, rb, LANES), f32)]
        + bufs
        + [pltpu.SemaphoreType.DMA((2 * (nz + ny - 2),)), pltpu.SemaphoreType.DMA((2 * (nz + ny - 2),))],
        compiler_params=pltpu.CompilerParams(collective_id=0, has_side_effects=True),
    )(xa, xb)


def per_device(ny, nz, proj, tiles, owner, lengths):
    view_count, group_rows, footprint = proj.shape
    samples = tiles.shape[2]
    group = lax.axis_index("chord")
    view_place = lax.axis_index("view")
    view_devices = ny * nz
    owned = group_rows // view_devices
    chunks_per_row = samples // LANES
    slots = min(chunks_per_row * owned, (PACK + owned * (LANES - 1)) // LANES)

    tile_rows = tiles.reshape(view_count, footprint, samples)
    sums = jnp.einsum("vkd,vds->ks", proj, tile_rows, preferred_element_type=jnp.float32)

    my_order = lax.dynamic_index_in_dim(owner, group, 0, keepdims=False)
    my_lengths = lax.dynamic_index_in_dim(lengths, group, 0, keepdims=False)
    order_len = pick(my_lengths[None, :], my_order[None, :])
    order_len = order_len.reshape(view_devices, owned)
    order_rows = my_order.reshape(view_devices, owned)

    counts = (order_len + LANES - 1) // LANES
    ends = jnp.cumsum(counts, axis=1)
    starts = ends - counts
    slot = jnp.arange(slots, dtype=jnp.int32)
    member = jnp.sum((ends[:, None, :] <= slot[None, :, None]).astype(jnp.int32), axis=2)
    member = jnp.minimum(member, owned - 1)
    first = pick(starts, member)
    src_row = pick(order_rows, member)
    within = jnp.clip(slot[None, :] - first, 0, chunks_per_row - 1)
    src = (src_row * chunks_per_row + within).reshape(ny, nz, slots)
    half = (slots + 1) // 2
    flat = sums.reshape(group_rows * chunks_per_row, LANES)
    xa = jnp.take(flat, src[:, :, :half].transpose(1, 0, 2), axis=0, mode="clip")
    xb = jnp.take(flat, src[:, :, half:], axis=0, mode="clip")

    mine = jnp.concatenate(reduce_scatter(xa, xb, ny, nz), axis=0)

    my_starts = lax.dynamic_index_in_dim(starts, view_place, 0, keepdims=False)
    my_len = lax.dynamic_index_in_dim(order_len, view_place, 0, keepdims=False)
    back = my_starts[:, None] + jnp.arange(chunks_per_row, dtype=jnp.int32)[None, :]
    back = jnp.minimum(back, slots - 1)
    rows = jnp.take(mine, back.reshape(-1), axis=0, mode="clip").reshape(owned, samples)

    table = kernel_table(samples, 0.0, samples)
    recon = invert_block(rows, my_len, table, 0.0)
    return recon[None]


def solution(mesh):
    view_devices = mesh.shape["view"]
    ny = int(round(math.sqrt(view_devices)))
    nz = view_devices // ny
    placed = (P("view", "chord", None), P("view", None, None), P(), P())
    return jax.shard_map(
        functools.partial(per_device, ny, nz),
        mesh=mesh,
        in_specs=placed,
        out_specs=P("chord", "view", None),
        check_vma=False,
    )
```

profile of v0, /device:TPU:6, one launch (start us, length us, event | category | flops | bytes accessed | tf_op | source)
XLA Modules:
  0.0 75.5 jit_solution(2095228952252430988)
XLA Ops:
  0.0 0.0 copy-start
  0.0 1.9 %copy-done = bf16[6,256,1024]{2,1,0:T(8,128)(2,1)S(1)} copy-done((bf16[6,256,1024]{2,1,0:T(8,128)(2,1)S(1)}, bf16[6,256,1024]{2,1,0:T(8,128)(2,1)}, u32[]{:S(2)}) %copy-start) | copy-done | bytes 3145752
  1.9 4.5 %convolution_bitcast_fusion = f32[512,1024]{1,0:T(8,128)} fusion(bf16[12,512,128]{2,1,0:T(8,128)(2,1)} %param.4, bf16[12,128,1024]{2,1,0:T(8,128)(2,1)S(1)} %bitcast.23), kind=kOutput, calls=%fused_computation.7 | convolution fusion | flops 1610612736 | bytes 6815744 | tf_op jit(solution)/shard_map/vkd,vds->ks/dot_general | solution.py:153
  6.4 2.7 %reshape.168 = f32[4096,128]{1,0:T(8,128)} reshape(f32[512,1024]{1,0:T(8,128)} %convolution_bitcast_fusion) | data formatting | bytes 4194304 | tf_op jit(solution)/shard_map/reshape | solution.py:172
  9.1 0.5 broadcast.156
  9.6 1.4 %fusion.26 = (s32[512]{0:T(512)S(1)}, s32[1,512]{1,0:T(1,128)S(1)}, s32[1,512]{1,0:T(1,128)S(1)}) fusion(s32[]{:T(128)} %broadcast.156, s32[8,512]{1,0:T(8,128)} %param.6, s32[]{:T(128)S(6)} %select_n.49, s32[8,512]{1,0:T(8,128)} %param.7), kind=kLoop, calls=%fused_computation.58 | loop fusion | bytes 10248 | tf_op jit(solution)/shard_map/jit(dynamic_index_in_dim)/dynamic_slice | solution.py:155
  11.0 0.1 broadcast_in_dim.76
  11.1 0.1 copy.7
  11.2 0.3 select_reduce_fusion
  11.4 0.1 reshape.166
  11.6 0.2 reduce_window_sum.11
  11.7 0.1 copy.6
  11.8 0.1 convert_reduce_fusion
  11.9 0.1 copy.9
  12.0 0.1 select_reduce_fusion.2
  12.1 0.1 copy.10
  12.2 0.1 copy.8
  12.4 0.1 reshape.172
  12.5 5.2 %gather_fusion = f32[1408,128]{1,0:T(8,128)} fusion(f32[4096,128]{1,0:T(8,128)} %reshape.168, s32[2048]{0:T(1024)S(1)} %pad_clamp_fusion.1), kind=kCustom, calls=%fused_computation | custom fusion | bytes 1447424 | tf_op jit(solution)/shard_map/jit(_take)/gather | solution.py:173
  17.7 2.1 %reshape.171.xa = f32[8,8,22,128]{3,2,1,0:T(8,128)} reshape(f32[1408,128]{1,0:T(8,128)} %gather_fusion) | data formatting | bytes 1441792 | tf_op jit(solution)/shard_map/jit(_take)/gather | solution.py:173
  19.8 0.1 slice.15
  19.9 0.1 reshape.180
  20.0 5.2 %gather_fusion.1 = f32[1344,128]{1,0:T(8,128)} fusion(f32[4096,128]{1,0:T(8,128)} %reshape.168, s32[2048]{0:T(1024)S(1)} %pad_clamp_fusion), kind=kCustom, calls=%fused_computation.1 | custom fusion | bytes 1381632 | tf_op jit(solution)/shard_map/jit(_take)/gather | solution.py:174
  25.2 2.0 %reshape.179.xb = f32[8,8,21,128]{3,2,1,0:T(8,128)} reshape(f32[1344,128]{1,0:T(8,128)} %gather_fusion.1) | data formatting | bytes 1376256 | tf_op jit(solution)/shard_map/jit(_take)/gather | solution.py:174
  27.3 44.1 %shard_map.46 = (f32[22,128]{1,0:T(8,128)}, f32[21,128]{1,0:T(8,128)}) custom-call(f32[8,8,22,128]{3,2,1,0:T(8,128)} %reshape.171.xa, f32[8,8,21,128]{3,2,1,0:T(8,128)} %reshape.179.xb), custom_call_target="tpu_custom_call" | custom-call | tf_op jit(solution)/shard_map/pallas_call | solution.py:130
  71.3 0.7 pad_maximum_fusion
  72.1 0.1 add_minimum_fusion
  72.2 0.1 reshape.188
  72.3 0.6 gather_fusion.2
  72.9 2.6 %fusion.5 = f32[1,8,1024]{2,1,0:T(8,128)} fusion(f32[8,1024]{1,0:T(8,128)S(1)} %reshape.169, f32[1024]{0:T(1024)S(1)} %iota_add_fusion, f32[8]{0:T(128)S(1)} %fusion.20), kind=kOutput, calls=%fused_computation.10 | convolution fusion | flops 53583872 | bytes 69664 | tf_op jit(solution)/shard_map/dot_general | solution.py:33
  (14 shorter events, 0.1 us)
Async XLA Ops:
  0.0 1.9 %copy-start = (bf16[6,256,1024]{2,1,0:T(8,128)(2,1)S(1)}, bf16[6,256,1024]{2,1,0:T(8,128)(2,1)}, u32[]{:S(2)}) copy-start(bf16[6,256,1024]{2,1,0:T(8,128)(2,1)} %param.5) | copy-start | bytes 9437188
where the time goes:
time: 76 us; the launch traced here: 75.5 us
  Pallas kernels  44.1 us (58%)
  local copies, waits for them, and re-layouts  22.7 us (30%)
  matrix products  7.08 us (9%)
  other arithmetic  1.55 us (2%)
    pallas_call x1, Pallas kernels, reduce_scatter(): pl.pallas_call(functools.partial(rs_kernel, ny, nz), out_shape=(jax.Shape...  44.1 us
    gather x2, local copies, waits for them, and re-layouts, per_device(): jnp.take(flat, src[:, :, :half].transpose(1, 0, 2), axis=0, mode='clip')  7.3 us
    gather x2, local copies, waits for them, and re-layouts, per_device(): xb = jnp.take(flat, src[:, :, half:], axis=0, mode='clip')  7.24 us
    dot_general x1, matrix products, per_device(): jnp.einsum('vkd,vds->ks', proj, tile_rows, preferred_element_type=jnp.flo...  4.49 us
    reshape x1, local copies, waits for them, and re-layouts, per_device(): flat = sums.reshape(group_rows * chunks_per_row, LANES)  2.74 us
    dot_general x1, matrix products, invert_block(): jnp.dot(scaled, table.T, precision=lax.Precision.HIGH, preferred_element_...  2.59 us
    dynamic_slice x2, local copies, waits for them, and re-layouts, per_device(): my_order = lax.dynamic_index_in_dim(owner, group, 0, keepdims=False)  1.91 us
    unnamed x2, local copies, waits for them, and re-layouts  1.89 us

commit v1 on v0

--- a/solution.py
+++ b/solution.py
@@ -170,8 +170,8 @@
     src = (src_row * chunks_per_row + within).reshape(ny, nz, slots)
     half = (slots + 1) // 2
     flat = sums.reshape(group_rows * chunks_per_row, LANES)
-    xa = jnp.take(flat, src[:, :, :half].transpose(1, 0, 2), axis=0, mode="clip")
-    xb = jnp.take(flat, src[:, :, half:], axis=0, mode="clip")
+    xa = jnp.take(flat, src[:, :, :half].transpose(1, 0, 2), axis=0, mode="wrap")
+    xb = jnp.take(flat, src[:, :, half:], axis=0, mode="wrap")
 
     mine = jnp.concatenate(reduce_scatter(xa, xb, ny, nz), axis=0)
 

time: 76 us -> 76 us (level)
  no operation moved by 1% of the time
where the time goes in v1:
time: 76 us; the launch traced here: 75.5 us
  Pallas kernels  44.1 us (58%)
  local copies, waits for them, and re-layouts  22.6 us (30%)
  matrix products  7.08 us (9%)
  other arithmetic  1.65 us (2%)
    pallas_call x1, Pallas kernels, reduce_scatter(): pl.pallas_call(functools.partial(rs_kernel, ny, nz), out_shape=(jax.Shape...  44.1 us
    gather x2, local copies, waits for them, and re-layouts, per_device(): jnp.take(flat, src[:, :, :half].transpose(1, 0, 2), axis=0, mode='wrap')  7.3 us
    gather x2, local copies, waits for them, and re-layouts, per_device(): xb = jnp.take(flat, src[:, :, half:], axis=0, mode='wrap')  7.24 us
    dot_general x1, matrix products, per_device(): jnp.einsum('vkd,vds->ks', proj, tile_rows, preferred_element_type=jnp.flo...  4.49 us
    reshape x1, local copies, waits for them, and re-layouts, per_device(): flat = sums.reshape(group_rows * chunks_per_row, LANES)  2.74 us
    dot_general x1, matrix products, invert_block(): jnp.dot(scaled, table.T, precision=lax.Precision.HIGH, preferred_element_...  2.59 us
    dynamic_slice x2, local copies, waits for them, and re-layouts, per_device(): my_order = lax.dynamic_index_in_dim(owner, group, 0, keepdims=False)  1.91 us
    unnamed x2, local copies, waits for them, and re-layouts  1.89 us

profile of v1, /device:TPU:6, one launch (start us, length us, event | category | flops | bytes accessed | tf_op | source)
XLA Modules:
  0.0 75.5 jit_solution(16027389938827310385)
XLA Ops:
  0.0 0.0 copy-start
  0.0 1.9 %copy-done = bf16[6,256,1024]{2,1,0:T(8,128)(2,1)S(1)} copy-done((bf16[6,256,1024]{2,1,0:T(8,128)(2,1)S(1)}, bf16[6,256,1024]{2,1,0:T(8,128)(2,1)}, u32[]{:S(2)}) %copy-start) | copy-done | bytes 3145752
  1.9 4.5 %convolution_bitcast_fusion = f32[512,1024]{1,0:T(8,128)} fusion(bf16[12,512,128]{2,1,0:T(8,128)(2,1)} %param.4, bf16[12,128,1024]{2,1,0:T(8,128)(2,1)S(1)} %bitcast.27), kind=kOutput, calls=%fused_computation.7 | convolution fusion | flops 1610612736 | bytes 6815744 | tf_op jit(solution)/shard_map/vkd,vds->ks/dot_general | solution.py:153
  6.4 2.7 %reshape.168 = f32[4096,128]{1,0:T(8,128)} reshape(f32[512,1024]{1,0:T(8,128)} %convolution_bitcast_fusion) | data formatting | bytes 4194304 | tf_op jit(solution)/shard_map/reshape | solution.py:172
  9.1 0.5 broadcast.174
  9.6 1.4 %fusion.28 = (s32[512]{0:T(512)S(1)}, s32[1,512]{1,0:T(1,128)S(1)}, s32[1,512]{1,0:T(1,128)S(1)}) fusion(s32[]{:T(128)} %broadcast.174, s32[8,512]{1,0:T(8,128)} %param.6, s32[]{:T(128)S(6)} %select_n.66, s32[8,512]{1,0:T(8,128)} %param.7), kind=kLoop, calls=%fused_computation.66 | loop fusion | bytes 10248 | tf_op jit(solution)/shard_map/jit(dynamic_index_in_dim)/dynamic_slice | solution.py:155
  11.0 0.1 broadcast_in_dim.76
  11.1 0.1 copy.7
  11.2 0.3 select_reduce_fusion
  11.4 0.1 reshape.166
  11.6 0.2 reduce_window_sum.11
  11.7 0.1 copy.6
  11.8 0.1 convert_reduce_fusion
  11.9 0.1 copy.9
  12.0 0.1 select_reduce_fusion.2
  12.1 0.1 copy.10
  12.2 0.1 copy.8
  12.4 0.1 reshape.172
  12.5 5.2 %gather_fusion = f32[1408,128]{1,0:T(8,128)} fusion(f32[4096,128]{1,0:T(8,128)} %reshape.168, s32[2048]{0:T(1024)S(1)} %pad_clamp_fusion.1), kind=kCustom, calls=%fused_computation | custom fusion | bytes 1447424 | tf_op jit(solution)/shard_map/jit(_take)/gather | solution.py:173
  17.7 2.1 %reshape.171.xa = f32[8,8,22,128]{3,2,1,0:T(8,128)} reshape(f32[1408,128]{1,0:T(8,128)} %gather_fusion) | data formatting | bytes 1441792 | tf_op jit(solution)/shard_map/jit(_take)/gather | solution.py:173
  19.8 0.1 add_select_fusion
  19.9 0.1 reshape.180
  20.1 5.2 %gather_fusion.1 = f32[1344,128]{1,0:T(8,128)} fusion(f32[4096,128]{1,0:T(8,128)} %reshape.168, s32[2048]{0:T(1024)S(1)} %pad_clamp_fusion), kind=kCustom, calls=%fused_computation.1 | custom fusion | bytes 1381632 | tf_op jit(solution)/shard_map/jit(_take)/gather | solution.py:174
  25.3 2.0 %reshape.179.xb = f32[8,8,21,128]{3,2,1,0:T(8,128)} reshape(f32[1344,128]{1,0:T(8,128)} %gather_fusion.1) | data formatting | bytes 1376256 | tf_op jit(solution)/shard_map/jit(_take)/gather | solution.py:174
  27.3 44.1 %shard_map.46 = (f32[22,128]{1,0:T(8,128)}, f32[21,128]{1,0:T(8,128)}) custom-call(f32[8,8,22,128]{3,2,1,0:T(8,128)} %reshape.171.xa, f32[8,8,21,128]{3,2,1,0:T(8,128)} %reshape.179.xb), custom_call_target="tpu_custom_call" | custom-call | tf_op jit(solution)/shard_map/pallas_call | solution.py:130
  71.4 0.7 pad_maximum_fusion
  72.1 0.1 add_minimum_fusion
  72.2 0.1 reshape.188
  72.3 0.6 gather_fusion.2
  72.9 2.6 %fusion.5 = f32[1,8,1024]{2,1,0:T(8,128)} fusion(f32[8,1024]{1,0:T(8,128)S(1)} %reshape.169, f32[1024]{0:T(1024)S(1)} %iota_add_fusion, f32[8]{0:T(128)S(1)} %fusion.22), kind=kOutput, calls=%fused_computation.10 | convolution fusion | flops 53583872 | bytes 69664 | tf_op jit(solution)/shard_map/dot_general | solution.py:33
  (14 shorter events, 0.2 us)
Async XLA Ops:
  0.0 1.9 %copy-start = (bf16[6,256,1024]{2,1,0:T(8,128)(2,1)S(1)}, bf16[6,256,1024]{2,1,0:T(8,128)(2,1)}, u32[]{:S(2)}) copy-start(bf16[6,256,1024]{2,1,0:T(8,128)(2,1)} %param.5) | copy-start | bytes 9437188

commit v2 on v1

--- a/solution.py
+++ b/solution.py
@@ -139,6 +139,55 @@
     )(xa, xb)
 
 
+def pack_kernel(ia_ref, ib_ref, proj_ref, tiles_ref, xa_ref, xb_ref, acc_ref):
+    blocks, pair, samples = tiles_ref.shape
+    footprint = proj_ref.shape[2]
+    per = pair // footprint
+    chunks = samples // LANES
+    width = min(samples, 256)
+    for cb in range(samples // width):
+        cols = pl.ds(cb * width, width)
+        total = None
+        for b in range(blocks):
+            lhs = jnp.concatenate([proj_ref[b * per + h] for h in range(per)], axis=1)
+            term = jnp.dot(lhs, tiles_ref[b, :, cols], preferred_element_type=jnp.float32)
+            total = term if total is None else total + term
+        acc_ref[:, cols] = total
+
+    for idx_ref, out_ref in ((ia_ref, xa_ref), (ib_ref, xb_ref)):
+        n0, n1, rows = out_ref.shape[:3]
+
+        def body(i, carry, idx_ref=idx_ref, out_ref=out_ref, n1=n1, rows=rows):
+            a = i // n1
+            c = lax.rem(i, n1)
+            for r in range(rows):
+                flat = idx_ref[i * rows + r]
+                row = flat // chunks
+                col = pl.multiple_of(lax.rem(flat, chunks) * LANES, LANES)
+                top = pl.multiple_of((row // 8) * 8, 8)
+                tile = acc_ref[pl.ds(top, 8), pl.ds(col, LANES)]
+                hit = lax.broadcasted_iota(jnp.int32, tile.shape, 0) == row - top
+                out_ref[a, c, pl.ds(r, 1), :] = jnp.sum(
+                    jnp.where(hit, tile, 0.0), axis=0, keepdims=True
+                )
+            return carry
+
+        lax.fori_loop(0, n0 * n1, body, 0)
+
+
+def pack(ia, ib, proj, tiles, shape_a, shape_b):
+    f32 = jnp.float32
+    samples = tiles.shape[2]
+    return pl.pallas_call(
+        pack_kernel,
+        out_shape=(jax.ShapeDtypeStruct(shape_a, f32), jax.ShapeDtypeStruct(shape_b, f32)),
+        in_specs=[pl.BlockSpec(memory_space=pltpu.SMEM)] * 2
+        + [pl.BlockSpec(memory_space=pltpu.VMEM)] * 2,
+        out_specs=(pl.BlockSpec(memory_space=pltpu.VMEM),) * 2,
+        scratch_shapes=[pltpu.VMEM((proj.shape[1], samples), f32)],
+    )(ia, ib, proj, tiles)
+
+
 def per_device(ny, nz, proj, tiles, owner, lengths):
     view_count, group_rows, footprint = proj.shape
     samples = tiles.shape[2]
@@ -149,8 +198,6 @@
     chunks_per_row = samples // LANES
     slots = min(chunks_per_row * owned, (PACK + owned * (LANES - 1)) // LANES)
 
-    tile_rows = tiles.reshape(view_count, footprint, samples)
-    sums = jnp.einsum("vkd,vds->ks", proj, tile_rows, preferred_element_type=jnp.float32)
 
     my_order = lax.dynamic_index_in_dim(owner, group, 0, keepdims=False)
     my_lengths = lax.dynamic_index_in_dim(lengths, group, 0, keepdims=False)
@@ -169,9 +216,10 @@
     within = jnp.clip(slot[None, :] - first, 0, chunks_per_row - 1)
     src = (src_row * chunks_per_row + within).reshape(ny, nz, slots)
     half = (slots + 1) // 2
-    flat = sums.reshape(group_rows * chunks_per_row, LANES)
-    xa = jnp.take(flat, src[:, :, :half].transpose(1, 0, 2), axis=0, mode="wrap")
-    xb = jnp.take(flat, src[:, :, half:], axis=0, mode="wrap")
+    ia = src[:, :, :half].transpose(1, 0, 2)
+    ib = src[:, :, half:]
+    xa, xb = pack(ia.reshape(-1), ib.reshape(-1), proj, tiles,
+                  ia.shape + (LANES,), ib.shape + (LANES,))
 
     mine = jnp.concatenate(reduce_scatter(xa, xb, ny, nz), axis=0)
 

time: 76 us -> 90.4 us (1.19)
  Pallas kernels: 44.1 us -> 81.1 us
  local copies, waits for them, and re-layouts: 22.6 us -> 4.7 us
  matrix products: 7.08 us -> 2.59 us
    pallas_call x0 -> x1, Pallas kernels: none -> 37 us  [pack(): pl.pallas_call(pack_kernel, out_shape=(jax.ShapeDtypeStruct(shape_a, f32)...]
    gather x4 -> x0, local copies, waits for them, and re-layouts: 14.5 us -> none  [the longest x2 7.3 us: per_device(): jnp.take(flat, src[:, :, :half].transpose(1, 0, 2), axis=0, mode='wrap')]
    dot_general x1 -> x0, matrix products: 4.49 us -> none  [per_device(): jnp.einsum('vkd,vds->ks', proj, tile_rows, preferred_element_type=jnp.flo...]
    unnamed x2 -> x0, local copies, waits for them, and re-layouts: 1.89 us -> none
    reshape x1 -> x2, local copies, waits for them, and re-layouts: 2.74 us -> 1.47 us  [the longest x1 0.74 us: per_device(): ib.reshape(-1)]
where the time goes in v2:
time: 90.4 us; the launch traced here: 90 us
  Pallas kernels  81.1 us (90%)
  local copies, waits for them, and re-layouts  4.7 us (5%)
  matrix products  2.59 us (3%)
  other arithmetic  1.52 us (2%)
    pallas_call x1, Pallas kernels, reduce_scatter(): pl.pallas_call(functools.partial(rs_kernel, ny, nz), out_shape=(jax.Shape...  44.1 us
    pallas_call x1, Pallas kernels, pack(): pl.pallas_call(pack_kernel, out_shape=(jax.ShapeDtypeStruct(shape_a, f32)...  37 us
    dot_general x1, matrix products, invert_block(): jnp.dot(scaled, table.T, precision=lax.Precision.HIGH, preferred_element_...  2.59 us
    dynamic_slice x2, local copies, waits for them, and re-layouts, per_device(): my_order = lax.dynamic_index_in_dim(owner, group, 0, keepdims=False)  1.91 us

profile of v2, /device:TPU:6, one launch (start us, length us, event | category | flops | bytes accessed | tf_op | source)
XLA Modules:
  0.0 90.0 jit_solution(12587406764094911223)
XLA Ops:
  0.0 0.5 broadcast.148
  0.5 1.4 %fusion.26 = (s32[512]{0:T(512)S(1)}, s32[1,512]{1,0:T(1,128)S(1)}, s32[1,512]{1,0:T(1,128)S(1)}) fusion(s32[]{:T(128)} %broadcast.148, s32[8,512]{1,0:T(8,128)} %param.6, s32[]{:T(128)S(6)} %select_n.49, s32[8,512]{1,0:T(8,128)} %param.7), kind=kLoop, calls=%fused_computation.53 | loop fusion | bytes 10248 | tf_op jit(solution)/shard_map/jit(dynamic_index_in_dim)/dynamic_slice | solution.py:202
  1.9 0.2 select_reduce_fusion
  2.2 0.1 reshape.166
  2.3 0.1 broadcast_in_dim.68
  2.4 0.1 copy.7
  2.5 0.2 reduce_window_sum.11
  2.7 0.1 copy.6
  2.8 0.1 copy.9
  2.8 0.1 add_minimum_fusion
  2.9 0.1 reshape.172
  3.0 0.1 convert_reduce_fusion
  3.1 0.1 select_reduce_fusion.2
  3.2 0.1 copy.8
  3.3 0.1 copy.10
  3.4 0.1 slice.11
  3.5 0.7 reshape.168.ib_ref
  4.2 0.7 reshape.167.ia_ref
  5.0 37.0 %shard_map.46 = (f32[8,8,22,128]{3,2,1,0:T(8,128)}, f32[8,8,21,128]{3,2,1,0:T(8,128)}) custom-call(s32[1408]{0:T(1024)} %reshape.167.ia_ref, s32[1344]{0:T(1024)} %reshape.168.ib_ref, bf16[12,512,128]{2,1,0:T(8,128)(2,1)} %proj_ref.1, bf16[6,256,1024]{2,1,0:T(8,128)(2,1)} %tiles_ref.1), custom_call_target="tpu_custom_call" | custom-call | tf_op jit(solution)/shard_map/pallas_call | solution.py:181
  42.0 44.1 %shard_map.47 = (f32[22,128]{1,0:T(8,128)}, f32[21,128]{1,0:T(8,128)}) custom-call(f32[8,8,22,128]{3,2,1,0:T(8,128)} %get-tuple-element.9.xa, f32[8,8,21,128]{3,2,1,0:T(8,128)} %get-tuple-element.10.xb), custom_call_target="tpu_custom_call" | custom-call | tf_op jit(solution)/shard_map/pallas_call | solution.py:130
  86.0 0.7 pad_maximum_fusion
  86.8 0.6 gather_fusion
  87.4 2.6 %fusion.5 = f32[1,8,1024]{2,1,0:T(8,128)} fusion(f32[8,1024]{1,0:T(8,128)S(1)} %reshape.169, f32[1024]{0:T(1024)S(1)} %iota_add_fusion, f32[8]{0:T(128)S(1)} %fusion.20), kind=kOutput, calls=%fused_computation.7 | convolution fusion | flops 53583872 | bytes 69664 | tf_op jit(solution)/shard_map/dot_general | solution.py:33
  (12 shorter events, 0.2 us)

commit v3 on v1

--- a/solution.py
+++ b/solution.py
@@ -149,14 +149,18 @@
     chunks_per_row = samples // LANES
     slots = min(chunks_per_row * owned, (PACK + owned * (LANES - 1)) // LANES)
 
-    tile_rows = tiles.reshape(view_count, footprint, samples)
-    sums = jnp.einsum("vkd,vds->ks", proj, tile_rows, preferred_element_type=jnp.float32)
-
     my_order = lax.dynamic_index_in_dim(owner, group, 0, keepdims=False)
     my_lengths = lax.dynamic_index_in_dim(lengths, group, 0, keepdims=False)
     order_len = pick(my_lengths[None, :], my_order[None, :])
     order_len = order_len.reshape(view_devices, owned)
-    order_rows = my_order.reshape(view_devices, owned)
+
+    perm = (my_order[:, None] == jnp.arange(group_rows, dtype=jnp.int32)[None, :]).astype(proj.dtype)
+    proj_ord = jnp.einsum("rk,vkd->vrd", perm, proj, preferred_element_type=jnp.float32)
+    proj_ord = proj_ord.astype(proj.dtype)
+    tile_rows = tiles.reshape(view_count, footprint, samples)
+    sums = jnp.einsum("vrd,vds->rs", proj_ord, tile_rows, preferred_element_type=jnp.float32)
+    blocks = sums.reshape(ny, nz, owned, chunks_per_row, LANES).transpose(0, 1, 3, 2, 4)
+    blocks = blocks.reshape(ny, nz, owned * chunks_per_row, LANES)
 
     counts = (order_len + LANES - 1) // LANES
     ends = jnp.cumsum(counts, axis=1)
@@ -165,13 +169,14 @@
     member = jnp.sum((ends[:, None, :] <= slot[None, :, None]).astype(jnp.int32), axis=2)
     member = jnp.minimum(member, owned - 1)
     first = pick(starts, member)
-    src_row = pick(order_rows, member)
     within = jnp.clip(slot[None, :] - first, 0, chunks_per_row - 1)
-    src = (src_row * chunks_per_row + within).reshape(ny, nz, slots)
+    src = (within * owned + member).reshape(ny, nz, slots)
     half = (slots + 1) // 2
-    flat = sums.reshape(group_rows * chunks_per_row, LANES)
-    xa = jnp.take(flat, src[:, :, :half].transpose(1, 0, 2), axis=0, mode="wrap")
-    xb = jnp.take(flat, src[:, :, half:], axis=0, mode="wrap")
+    choose = (src[..., None] == jnp.arange(owned * chunks_per_row, dtype=jnp.int32)).astype(jnp.float32)
+    xa = jnp.einsum("yzbj,yzjl->zybl", choose[:, :, :half], blocks,
+                    precision=lax.Precision.HIGHEST, preferred_element_type=jnp.float32)
+    xb = jnp.einsum("yzbj,yzjl->yzbl", choose[:, :, half:], blocks,
+                    precision=lax.Precision.HIGHEST, preferred_element_type=jnp.float32)
 
     mine = jnp.concatenate(reduce_scatter(xa, xb, ny, nz), axis=0)
 
@@ -179,7 +184,7 @@
     my_len = lax.dynamic_index_in_dim(order_len, view_place, 0, keepdims=False)
     back = my_starts[:, None] + jnp.arange(chunks_per_row, dtype=jnp.int32)[None, :]
     back = jnp.minimum(back, slots - 1)
-    rows = jnp.take(mine, back.reshape(-1), axis=0, mode="clip").reshape(owned, samples)
+    rows = jnp.take(mine, back.reshape(-1), axis=0).reshape(owned, samples)
 
     table = kernel_table(samples, 0.0, samples)
     recon = invert_block(rows, my_len, table, 0.0)

time: 76 us -> 66.9 us (0.88)
  local copies, waits for them, and re-layouts: 22.6 us -> 7.54 us
  matrix products: 7.08 us -> 12.6 us
    gather x5 -> x2, local copies, waits for them, and re-layouts: 15.1 us -> 0.61 us  [per_device(): rows = jnp.take(mine, back.reshape(-1), axis=0).reshape(owned, samples)]
    dot_general x1 -> x4, matrix products: 4.49 us -> 10 us  [the longest x1 3.69 us: per_device(): jnp.einsum('yzbj,yzjl->zybl', choose[:, :, :half], blocks, precision=lax....]
    dot_general x0 -> x1, local copies, waits for them, and re-layouts: none -> 4.76 us  [per_device(): jnp.einsum('vrd,vds->rs', proj_ord, tile_rows, preferred_element_type=jnp...]
    reshape x2 -> x0, local copies, waits for them, and re-layouts: 2.75 us -> none  [the longest x1 2.74 us: per_device(): flat = sums.reshape(group_rows * chunks_per_row, LANES)]
    dynamic_slice x2 -> x1, local copies, waits for them, and re-layouts: 1.91 us -> 0.74 us  [per_device(): my_lengths = lax.dynamic_index_in_dim(lengths, group, 0, keepdims=False)]
    unnamed x2 -> x6, local copies, waits for them, and re-layouts: 1.89 us -> 0.85 us
where the time goes in v3:
time: 66.9 us; the launch traced here: 66.5 us
  Pallas kernels  44.1 us (66%)
  matrix products  12.6 us (19%)
  local copies, waits for them, and re-layouts  7.54 us (11%)
  other arithmetic  2.13 us (3%)
    pallas_call x1, Pallas kernels, reduce_scatter(): pl.pallas_call(functools.partial(rs_kernel, ny, nz), out_shape=(jax.Shape...  44.1 us
    dot_general x1, local copies, waits for them, and re-layouts, per_device(): jnp.einsum('vrd,vds->rs', proj_ord, tile_rows, preferred_element_type=jnp...  4.76 us
    dot_general x1, matrix products, per_device(): jnp.einsum('yzbj,yzjl->zybl', choose[:, :, :half], blocks, precision=lax....  3.69 us
    dot_general x1, matrix products, per_device(): jnp.einsum('vrd,vds->rs', proj_ord, tile_rows, preferred_element_type=jnp...  3.18 us
    dot_general x1, matrix products, invert_block(): jnp.dot(scaled, table.T, precision=lax.Precision.HIGH, preferred_element_...  2.59 us
    dot_general x1, matrix products, per_device(): jnp.einsum('yzbj,yzjl->yzbl', choose[:, :, half:], blocks, precision=lax....  2.13 us

profile of v3, /device:TPU:6, one launch (start us, length us, event | category | flops | bytes accessed | tf_op | source)
XLA Modules:
  0.0 66.5 jit_solution(800082077598942436)
XLA Ops:
  0.0 0.0 copy-start
  0.0 4.8 %copy.28 = bf16[1024,128,12]{1,0,2:T(8,128)(2,1)} copy(bf16[1024,128,12]{0,1,2:T(8,128)(2,1)} %bitcast.48) | data formatting | bytes 6291456 | tf_op jit(solution)/shard_map/vrd,vds->rs/dot_general | solution.py:161
  4.8 0.7 %constant_dynamic-slice_fusion.2 = (s32[1,512]{1,0:T(1,128)S(1)}, s32[1,512]{1,0:T(1,128)S(1)}) fusion(s32[8,512]{1,0:T(8,128)} %param.7, s32[]{:T(128)S(6)} %select_n.68, s32[8,512]{1,0:T(8,128)} %param.6), kind=kLoop, calls=%fused_computation.63 | loop fusion | bytes 8196 | tf_op jit(solution)/shard_map/jit(dynamic_index_in_dim)/dynamic_slice | solution.py:153
  5.5 0.0 copy-done
  5.5 0.0 copy-start.2
  5.5 1.0 %convolution_convert_fusion = bf16[512,12,128]{2,0,1:T(8,128)(2,1)S(1)} fusion(bf16[12,512,128]{2,1,0:T(8,128)(2,1)S(1)} %copy-done, s32[512]{0:T(512)S(1)} %bitcast.51), kind=kOutput, calls=%fused_computation.9 | convolution fusion | flops 806354944 | bytes 3147776 | tf_op jit(solution)/shard_map/rk,vkd->vrd/dot_general | solution.py:158
  6.6 0.8 %copy-done.2 = bf16[1024,128,12]{1,0,2:T(8,128)(2,1)S(1)} copy-done((bf16[1024,128,12]{1,0,2:T(8,128)(2,1)S(1)}, bf16[1024,128,12]{1,0,2:T(8,128)(2,1)}, u32[]{:S(2)}) %copy-start.2) | copy-done | bytes 3145752
  7.4 3.2 %fusion.7 = f32[8,8,64,128]{3,2,1,0:T(8,128)} fusion(bf16[8,128,128,12,1,1]{2,1,0,3,5,4:T(8,128)(2,1)S(1)} %bitcast.49, bf16[8,8,8,128,12,1]{3,2,1,0,4,5:T(8,128)(2,1)S(1)} %bitcast.53), kind=kOutput, calls=%fused_computation.10 | convolution fusion | flops 1610612736 | bytes 6815744 | tf_op jit(solution)/shard_map/vrd,vds->rs/dot_general | solution.py:161
  10.6 0.2 select_reduce_fusion
  10.8 0.1 reshape.196
  11.0 0.2 reduce_window_sum.11
  11.1 0.1 copy.23
  11.2 0.1 convert_reduce_fusion
  11.3 0.1 copy.26
  11.4 0.1 copy.24
  11.5 0.1 select_reduce_fusion.1
  11.5 0.1 copy.25
  11.6 0.0 copy-start.1
  11.7 0.6 iota_compare_fusion
  12.3 3.7 %fusion.3.xa = f32[8,8,22,128]{3,2,1,0:T(8,128)} fusion(f32[8,8,64,128]{3,2,1,0:T(8,128)} %fusion.7, pred[8,8,43,64]{3,2,0,1:T(8,128)(4,1)S(1)} %iota_compare_fusion), kind=kOutput, calls=%fused_computation.5 | convolution fusion | flops 138412032 | bytes 3014656 | tf_op jit(solution)/shard_map/yzbj,yzjl->zybl/dot_general | solution.py:176
  16.0 0.0 copy-done.1
  16.0 2.1 %fusion.17.xb = f32[8,8,21,128]{3,2,1,0:T(8,128)} fusion(f32[8,8,64,128]{3,2,1,0:T(8,128)S(1)} %copy-done.1, pred[8,8,43,64]{3,2,0,1:T(8,128)(4,1)S(1)} %iota_compare_fusion), kind=kOutput, calls=%fused_computation.21 | convolution fusion | flops 132120576 | bytes 2981888 | tf_op jit(solution)/shard_map/yzbj,yzjl->yzbl/dot_general | solution.py:178
  18.1 44.1 %shard_map.46 = (f32[22,128]{1,0:T(8,128)}, f32[21,128]{1,0:T(8,128)}) custom-call(f32[8,8,22,128]{3,2,1,0:T(8,128)} %fusion.3.xa, f32[8,8,21,128]{3,2,1,0:T(8,128)} %fusion.17.xb), custom_call_target="tpu_custom_call" | custom-call | tf_op jit(solution)/shard_map/pallas_call | solution.py:130
  62.2 0.7 %pad_maximum_fusion = f32[43,128]{1,0:T(8,128)S(1)} fusion(f32[21,128]{1,0:T(8,128)} %get-tuple-element.8, f32[22,128]{1,0:T(8,128)} %get-tuple-element.7), kind=kLoop, calls=%fused_computation.47 | loop fusion | flops 5504 | bytes 44032 | tf_op jit(solution)/shard_map/concatenate | solution.py:181
  62.9 0.1 add_minimum_fusion
  63.0 0.1 min.52
  63.1 0.6 gather_fusion
  63.7 0.1 compare_and_fusion
  63.8 0.1 copy.22
  63.9 2.6 %fusion.13 = f32[1,8,1024]{2,1,0:T(8,128)} fusion(f32[8,1024]{1,0:T(8,128)S(1)} %gather.7, f32[1024]{0:T(1024)S(1)} %iota_add_fusion, f32[8]{0:T(128)S(1)} %fusion.38, pred[8,8]{0,1:T(8,128)(4,1)S(1)} %copy.22), kind=kOutput, calls=%fused_computation.15 | convolution fusion | flops 53592064 | bytes 69728 | tf_op jit(solution)/shard_map/dot_general | solution.py:33
  (11 shorter events, 0.1 us)
Async XLA Ops:
  0.0 5.5 %copy-start = (bf16[12,512,128]{2,1,0:T(8,128)(2,1)S(1)}, bf16[12,512,128]{2,1,0:T(8,128)(2,1)}, u32[]{:S(2)}) copy-start(bf16[12,512,128]{2,1,0:T(8,128)(2,1)} %param.4) | copy-start | bytes 4718596
  5.5 1.9 %copy-start.2 = (bf16[1024,128,12]{1,0,2:T(8,128)(2,1)S(1)}, bf16[1024,128,12]{1,0,2:T(8,128)(2,1)}, u32[]{:S(2)}) copy-start(bf16[1024,128,12]{1,0,2:T(8,128)(2,1)} %copy.28) | copy-start | bytes 9437188
  11.6 4.3 %copy-start.1 = (f32[8,8,64,128]{3,2,1,0:T(8,128)S(1)}, f32[8,8,64,128]{3,2,1,0:T(8,128)}, u32[]{:S(2)}) copy-start(f32[8,8,64,128]{3,2,1,0:T(8,128)} %fusion.7) | copy-start | bytes 6291460

commit v4 on v3

--- a/solution.py
+++ b/solution.py
@@ -139,6 +139,34 @@
     )(xa, xb)
 
 
+def sums_kernel(perm_ref, proj_ref, tiles_ref, out_ref):
+    blocks, pair, samples = tiles_ref.shape
+    footprint = proj_ref.shape[2]
+    per = pair // footprint
+    perm = perm_ref[...]
+    total = None
+    for b in range(blocks):
+        lhs = jnp.concatenate(
+            [
+                jnp.dot(perm, proj_ref[b * per + h], preferred_element_type=jnp.float32)
+                for h in range(per)
+            ],
+            axis=1,
+        ).astype(proj_ref.dtype)
+        term = jnp.dot(lhs, tiles_ref[b], preferred_element_type=jnp.float32)
+        total = term if total is None else total + term
+    out_ref[...] = total
+
+
+def owner_sums(perm, proj, tiles):
+    return pl.pallas_call(
+        sums_kernel,
+        out_shape=jax.ShapeDtypeStruct((proj.shape[1], tiles.shape[2]), jnp.float32),
+        in_specs=[pl.BlockSpec(memory_space=pltpu.VMEM)] * 3,
+        out_specs=pl.BlockSpec(memory_space=pltpu.VMEM),
+    )(perm, proj, tiles)
+
+
 def per_device(ny, nz, proj, tiles, owner, lengths):
     view_count, group_rows, footprint = proj.shape
     samples = tiles.shape[2]
@@ -155,12 +183,8 @@
     order_len = order_len.reshape(view_devices, owned)
 
     perm = (my_order[:, None] == jnp.arange(group_rows, dtype=jnp.int32)[None, :]).astype(proj.dtype)
-    proj_ord = jnp.einsum("rk,vkd->vrd", perm, proj, preferred_element_type=jnp.float32)
-    proj_ord = proj_ord.astype(proj.dtype)
-    tile_rows = tiles.reshape(view_count, footprint, samples)
-    sums = jnp.einsum("vrd,vds->rs", proj_ord, tile_rows, preferred_element_type=jnp.float32)
-    blocks = sums.reshape(ny, nz, owned, chunks_per_row, LANES).transpose(0, 1, 3, 2, 4)
-    blocks = blocks.reshape(ny, nz, owned * chunks_per_row, LANES)
+    sums = owner_sums(perm, proj, tiles)
+    blocks = sums.reshape(ny, nz, owned, chunks_per_row, LANES)
 
     counts = (order_len + LANES - 1) // LANES
     ends = jnp.cumsum(counts, axis=1)
@@ -170,12 +194,16 @@
     member = jnp.minimum(member, owned - 1)
     first = pick(starts, member)
     within = jnp.clip(slot[None, :] - first, 0, chunks_per_row - 1)
-    src = (within * owned + member).reshape(ny, nz, slots)
+    member = member.reshape(ny, nz, slots)
+    within = within.reshape(ny, nz, slots)
     half = (slots + 1) // 2
-    choose = (src[..., None] == jnp.arange(owned * chunks_per_row, dtype=jnp.int32)).astype(jnp.float32)
-    xa = jnp.einsum("yzbj,yzjl->zybl", choose[:, :, :half], blocks,
+    choose = (
+        (member[..., None, None] == jnp.arange(owned, dtype=jnp.int32)[:, None])
+        & (within[..., None, None] == jnp.arange(chunks_per_row, dtype=jnp.int32)[None, :])
+    ).astype(jnp.float32)
+    xa = jnp.einsum("yzbmc,yzmcl->zybl", choose[:, :, :half], blocks,
                     precision=lax.Precision.HIGHEST, preferred_element_type=jnp.float32)
-    xb = jnp.einsum("yzbj,yzjl->yzbl", choose[:, :, half:], blocks,
+    xb = jnp.einsum("yzbmc,yzmcl->yzbl", choose[:, :, half:], blocks,
                     precision=lax.Precision.HIGHEST, preferred_element_type=jnp.float32)
 
     mine = jnp.concatenate(reduce_scatter(xa, xb, ny, nz), axis=0)

time: 66.9 us -> 67.2 us (level)
  Pallas kernels: 44.1 us -> 51.4 us
  local copies, waits for them, and re-layouts: 7.54 us -> 1.93 us
  matrix products: 12.6 us -> 10.4 us
  other arithmetic: 2.13 us -> 2.94 us
    pallas_call x0 -> x1, Pallas kernels: none -> 7.31 us  [owner_sums(): pl.pallas_call(sums_kernel, out_shape=jax.ShapeDtypeStruct((proj.shape[1]...]
    dot_general x1 -> x0, local copies, waits for them, and re-layouts: 4.76 us -> none  [per_device(): jnp.einsum('vrd,vds->rs', proj_ord, tile_rows, preferred_element_type=jnp...]
    dot_general x4 -> x2, matrix products: 10 us -> 7.81 us  [the longest x1 5.03 us: per_device(): jnp.einsum('yzbmc,yzmcl->yzbl', choose[:, :, half:], blocks, precision=la...]
    convert_element_type x0 -> x1, other arithmetic: none -> 0.95 us  [per_device(): (my_order[:, None] == jnp.arange(group_rows, dtype=jnp.int32)[None, :]).a...]
    unnamed x6 -> x2, local copies, waits for them, and re-layouts: 0.85 us -> 0.01 us
where the time goes in v4:
time: 67.2 us; the launch traced here: 66.8 us
  Pallas kernels  51.4 us (76%)
  matrix products  10.4 us (15%)
  other arithmetic  2.94 us (4%)
  local copies, waits for them, and re-layouts  1.93 us (3%)
    pallas_call x1, Pallas kernels, reduce_scatter(): pl.pallas_call(functools.partial(rs_kernel, ny, nz), out_shape=(jax.Shape...  44.1 us
    pallas_call x1, Pallas kernels, owner_sums(): pl.pallas_call(sums_kernel, out_shape=jax.ShapeDtypeStruct((proj.shape[1]...  7.31 us
    dot_general x1, matrix products, per_device(): jnp.einsum('yzbmc,yzmcl->yzbl', choose[:, :, half:], blocks, precision=la...  5.03 us
    dot_general x1, matrix products, per_device(): jnp.einsum('yzbmc,yzmcl->zybl', choose[:, :, :half], blocks, precision=la...  2.78 us
    dot_general x1, matrix products, invert_block(): jnp.dot(scaled, table.T, precision=lax.Precision.HIGH, preferred_element_...  2.59 us

profile of v4, /device:TPU:6, one launch (start us, length us, event | category | flops | bytes accessed | tf_op | source)
XLA Modules:
  0.0 66.8 jit_solution(12337691463519111291)
XLA Ops:
  0.0 0.7 %constant_dynamic-slice_fusion.2 = (s32[1,512]{1,0:T(1,128)S(1)}, s32[1,512]{1,0:T(1,128)S(1)}) fusion(s32[8,512]{1,0:T(8,128)} %param.7, s32[]{:T(128)S(6)} %select_n.68, s32[8,512]{1,0:T(8,128)} %param.6), kind=kLoop, calls=%fused_computation.59 | loop fusion | bytes 8196 | tf_op jit(solution)/shard_map/jit(dynamic_index_in_dim)/dynamic_slice | solution.py:181
  0.7 0.2 select_reduce_fusion
  1.0 0.1 reshape.202
  1.1 0.2 reduce_window_sum.11
  1.4 0.1 copy.14
  1.4 0.1 copy.17
  1.5 0.1 compare_and_fusion
  1.6 0.1 copy.13
  1.6 0.1 add_minimum_fusion
  1.7 0.1 min.52
  1.8 0.1 convert_reduce_fusion
  1.9 0.1 select_reduce_fusion.1
  2.0 0.1 copy.15
  2.1 0.1 copy.18
  2.3 0.4 broadcast_and_fusion
  2.7 1.0 %fusion.19.perm_ref = bf16[512,512]{1,0:T(8,128)(2,1)} fusion(s32[512]{0:T(512)S(1)} %bitcast.32), kind=kLoop, calls=%fused_computation.18 | loop fusion | flops 524288 | bytes 526336 | tf_op jit(solution)/shard_map/convert_element_type | solution.py:185
  3.6 7.3 %shard_map.46 = f32[512,1024]{1,0:T(8,128)} custom-call(bf16[512,512]{1,0:T(8,128)(2,1)} %fusion.19.perm_ref, bf16[12,512,128]{2,1,0:T(8,128)(2,1)} %proj_ref.1, bf16[6,256,1024]{2,1,0:T(8,128)(2,1)} %tiles_ref.1), custom_call_target="tpu_custom_call" | custom-call | tf_op jit(solution)/shard_map/pallas_call | solution.py:162
  11.0 0.0 copy-start
  11.0 5.0 %fusion.8.xb = f32[8,8,21,128]{3,2,1,0:T(8,128)} fusion(f32[8,8,8,8,128]{4,2,3,1,0:T(8,128)} %bitcast.28, pred[8,8,43,8,8]{2,3,4,0,1:T(8,128)(4,1)S(1)} %broadcast_and_fusion), kind=kOutput, calls=%fused_computation.10 | convolution fusion | flops 132120576 | bytes 2961408 | tf_op jit(solution)/shard_map/yzbmc,yzmcl->yzbl/dot_general | solution.py:206
  16.0 0.0 copy-done
  16.0 2.8 %fusion.11.xa = f32[8,8,22,128]{3,2,1,0:T(8,128)} fusion(f32[8,8,8,8,128]{4,2,3,1,0:T(8,128)S(1)} %bitcast.29, pred[8,8,43,8,8]{2,3,4,0,1:T(8,128)(4,1)S(1)} %broadcast_and_fusion), kind=kOutput, calls=%fused_computation.11 | convolution fusion | flops 138412032 | bytes 2994176 | tf_op jit(solution)/shard_map/yzbmc,yzmcl->zybl/dot_general | solution.py:204
  18.8 44.1 %shard_map.47 = (f32[22,128]{1,0:T(8,128)}, f32[21,128]{1,0:T(8,128)}) custom-call(f32[8,8,22,128]{3,2,1,0:T(8,128)} %fusion.11.xa, f32[8,8,21,128]{3,2,1,0:T(8,128)} %fusion.8.xb), custom_call_target="tpu_custom_call" | custom-call | tf_op jit(solution)/shard_map/pallas_call | solution.py:130
  62.8 0.7 %pad_maximum_fusion = f32[43,128]{1,0:T(8,128)S(1)} fusion(f32[21,128]{1,0:T(8,128)} %get-tuple-element.8, f32[22,128]{1,0:T(8,128)} %get-tuple-element.7), kind=kLoop, calls=%fused_computation.43 | loop fusion | flops 5504 | bytes 44032 | tf_op jit(solution)/shard_map/concatenate | solution.py:209
  63.6 0.6 gather_fusion
  64.2 2.6 %fusion.18 = f32[1,8,1024]{2,1,0:T(8,128)} fusion(f32[8,1024]{1,0:T(8,128)S(1)} %gather.7, f32[1024]{0:T(1024)S(1)} %iota_add_fusion, f32[8]{0:T(128)S(1)} %fusion.37, pred[8,8]{0,1:T(8,128)(4,1)S(1)} %copy.13), kind=kOutput, calls=%fused_computation.14 | convolution fusion | flops 53592064 | bytes 69728 | tf_op jit(solution)/shard_map/dot_general | solution.py:33
  (14 shorter events, 0.2 us)
Async XLA Ops:
  11.0 5.0 %copy-start = (f32[512,1024]{1,0:T(8,128)S(1)}, f32[512,1024]{1,0:T(8,128)}, u32[]{:S(2)}) copy-start(f32[512,1024]{1,0:T(8,128)} %shard_map.46) | copy-start | bytes 6291460

commit v5 on v4

--- a/solution.py
+++ b/solution.py
@@ -201,10 +201,17 @@
         (member[..., None, None] == jnp.arange(owned, dtype=jnp.int32)[:, None])
         & (within[..., None, None] == jnp.arange(chunks_per_row, dtype=jnp.int32)[None, :])
     ).astype(jnp.float32)
-    xa = jnp.einsum("yzbmc,yzmcl->zybl", choose[:, :, :half], blocks,
-                    precision=lax.Precision.HIGHEST, preferred_element_type=jnp.float32)
-    xb = jnp.einsum("yzbmc,yzmcl->yzbl", choose[:, :, half:], blocks,
-                    precision=lax.Precision.HIGHEST, preferred_element_type=jnp.float32)
+    bf16 = jnp.bfloat16
+    hi = lax.reduce_precision(blocks, exponent_bits=8, mantissa_bits=7)
+    rest = blocks - hi
+    mid = lax.reduce_precision(rest, exponent_bits=8, mantissa_bits=7)
+    lo = rest - mid
+    parts = jnp.stack([hi, mid, lo]).astype(bf16)
+    choose = choose.astype(bf16)
+    xa = jnp.einsum("yzbmc,pyzmcl->pzybl", choose[:, :, :half], parts,
+                    preferred_element_type=jnp.float32).sum(axis=0)
+    xb = jnp.einsum("yzbmc,pyzmcl->pyzbl", choose[:, :, half:], parts,
+                    preferred_element_type=jnp.float32).sum(axis=0)
 
     mine = jnp.concatenate(reduce_scatter(xa, xb, ny, nz), axis=0)
 

time: 67.2 us -> 65.9 us (0.981)
  matrix products: 10.4 us -> 6.67 us
  other arithmetic: 2.94 us -> 5.43 us
    dot_general x2, matrix products: 7.81 us -> 4.08 us  [the longest x1 2.43 us: per_device(): jnp.einsum('yzbmc,pyzmcl->pyzbl', choose[:, :, half:], parts, preferred_e...]
    another operation x0 -> x1, other arithmetic: none -> 2.48 us
where the time goes in v5:
time: 65.9 us; the launch traced here: 65.5 us
  Pallas kernels  51.4 us (78%)
  matrix products  6.67 us (10%)
  other arithmetic  5.43 us (8%)
  local copies, waits for them, and re-layouts  1.93 us (3%)
    pallas_call x1, Pallas kernels, reduce_scatter(): pl.pallas_call(functools.partial(rs_kernel, ny, nz), out_shape=(jax.Shape...  44.1 us
    pallas_call x1, Pallas kernels, owner_sums(): pl.pallas_call(sums_kernel, out_shape=jax.ShapeDtypeStruct((proj.shape[1]...  7.31 us
    dot_general x1, matrix products, invert_block(): jnp.dot(scaled, table.T, precision=lax.Precision.HIGH, preferred_element_...  2.59 us
    another operation x1, other arithmetic  2.48 us
    dot_general x1, matrix products, per_device(): jnp.einsum('yzbmc,pyzmcl->pyzbl', choose[:, :, half:], parts, preferred_e...  2.43 us
    dot_general x1, matrix products, per_device(): jnp.einsum('yzbmc,pyzmcl->pzybl', choose[:, :, :half], parts, preferred_e...  1.65 us

profile of v5, /device:TPU:6, one launch (start us, length us, event | category | flops | bytes accessed | tf_op | source)
XLA Modules:
  0.0 65.5 jit_solution(12815752428952194300)
XLA Ops:
  0.0 0.7 %constant_dynamic-slice_fusion.2 = (s32[1,512]{1,0:T(1,128)S(1)}, s32[1,512]{1,0:T(1,128)S(1)}) fusion(s32[8,512]{1,0:T(8,128)} %param.7, s32[]{:T(128)S(6)} %select_n.68, s32[8,512]{1,0:T(8,128)} %param.6), kind=kLoop, calls=%fused_computation.65 | loop fusion | bytes 8196 | tf_op jit(solution)/shard_map/jit(dynamic_index_in_dim)/dynamic_slice | solution.py:181
  0.7 0.2 select_reduce_fusion
  1.0 0.1 reshape.238
  1.1 0.2 reduce_window_sum.11
  1.4 0.1 copy.20
  1.4 0.1 copy.23
  1.5 0.1 compare_and_fusion
  1.6 0.1 copy.17
  1.6 0.1 add_minimum_fusion
  1.7 0.1 min.52
  1.8 0.1 convert_reduce_fusion
  1.9 0.1 select_reduce_fusion.1
  2.0 0.1 copy.21
  2.1 0.1 copy.24
  2.3 1.0 %fusion.12.perm_ref = bf16[512,512]{1,0:T(8,128)(2,1)} fusion(s32[512]{0:T(512)S(1)} %bitcast.43), kind=kLoop, calls=%fused_computation.25 | loop fusion | flops 524288 | bytes 526336 | tf_op jit(solution)/shard_map/convert_element_type | solution.py:185
  3.3 0.4 convert_convert_fusion
  3.7 7.3 %shard_map.46 = f32[512,1024]{1,0:T(8,128)} custom-call(bf16[512,512]{1,0:T(8,128)(2,1)} %fusion.12.perm_ref, bf16[12,512,128]{2,1,0:T(8,128)(2,1)} %proj_ref.1, bf16[6,256,1024]{2,1,0:T(8,128)(2,1)} %tiles_ref.1), custom_call_target="tpu_custom_call" | custom-call | tf_op jit(solution)/shard_map/pallas_call | solution.py:162
  11.0 2.5 %reduce-precision_convert_fusion.1 = (bf16[1,8,8,8,8,128]{5,3,4,0,1,2:T(8,128)(2,1)S(1)}, bf16[1,8,8,8,8,128]{5,3,4,0,1,2:T(8,128)(2,1)S(1)}, bf16[1,8,8,8,8,128]{5,3,4,0,1,2:T(8,128)(2,1)S(1)}) fusion(f32[1,8,8,8,8,128]{5,3,4,2,1,0:T(8,128)} %bitcast.38), kind=kLoop, calls=%fused_computation.9 | loop fusion | flops 3670016 | bytes 5242880 | tf_op jit(solution)/shard_map/convert
  13.5 1.6 %bitcast_reduce_fusion.1 = f32[8,8,128,22]{2,3,1,0:T(8,128)} fusion(bf16[8,8,43,8,8]{2,3,4,0,1:T(8,128)(2,1)S(1)} %convert_convert_fusion, bf16[1,8,8,8,8,128]{5,3,4,0,1,2:T(8,128)(2,1)S(1)} %get-tuple-element.10, bf16[1,8,8,8,8,128]{5,3,4,0,1,2:T(8,128)(2,1)S(1)} %get-tuple-element.11, bf16[1,8,8,8,8,128]{5,3,4,0,1,2:T(8,128)(2,1)S(1)} %get-tuple-element.9), kind=kOutput, calls=%fused_computation.11 | convolution fusion | flops 72712192 | bytes 4218880 | tf_op jit(solution)/shard_map/yzbmc,pyzmcl->pzybl/dot_general | solution.py:211
  15.1 2.4 %bitcast_reduce_fusion = f32[8,8,128,21]{2,3,1,0:T(8,128)} fusion(bf16[1,8,8,8,8,128]{5,3,4,0,1,2:T(8,128)(2,1)S(1)} %get-tuple-element.10, bf16[1,8,8,8,8,128]{5,3,4,0,1,2:T(8,128)(2,1)S(1)} %get-tuple-element.11, bf16[1,8,8,8,8,128]{5,3,4,0,1,2:T(8,128)(2,1)S(1)} %get-tuple-element.9, bf16[8,8,43,8,8]{2,3,4,0,1:T(8,128)(2,1)S(1)} %convert_convert_fusion), kind=kOutput, calls=%fused_computation.10 | convolution fusion | flops 69550080 | bytes 4186112 | tf_op jit(solution)/shard_map/yzbmc,pyzmcl->pyzbl/dot_general | solution.py:213
  17.5 44.1 %shard_map.47 = (f32[22,128]{1,0:T(8,128)}, f32[21,128]{1,0:T(8,128)}) custom-call(f32[8,8,22,128]{3,2,1,0:T(8,128)} %bitcast.39, f32[8,8,21,128]{3,2,1,0:T(8,128)} %bitcast.40), custom_call_target="tpu_custom_call" | custom-call | tf_op jit(solution)/shard_map/pallas_call | solution.py:130
  61.6 0.7 %pad_maximum_fusion.1 = f32[43,128]{1,0:T(8,128)S(1)} fusion(f32[21,128]{1,0:T(8,128)} %get-tuple-element.8, f32[22,128]{1,0:T(8,128)} %get-tuple-element.7), kind=kLoop, calls=%fused_computation.49 | loop fusion | flops 5504 | bytes 44032 | tf_op jit(solution)/shard_map/concatenate | solution.py:216
  62.3 0.6 gather_fusion
  62.9 2.6 %fusion.10 = f32[1,8,1024]{2,1,0:T(8,128)} fusion(f32[8,1024]{1,0:T(8,128)S(1)} %gather.7, f32[1024]{0:T(1024)S(1)} %iota_add_fusion, f32[8]{0:T(128)S(1)} %fusion.30, pred[8,8]{0,1:T(8,128)(4,1)S(1)} %copy.17), kind=kOutput, calls=%fused_computation.18 | convolution fusion | flops 53592064 | bytes 69728 | tf_op jit(solution)/shard_map/dot_general | solution.py:33
  (14 shorter events, 0.2 us)

commit v6 on v5

--- a/solution.py
+++ b/solution.py
@@ -76,6 +76,26 @@
     return [(r["rr"].at[r["n"] // 2 - 1], r["rl"].at[r["n"] - 2 - r["n"] // 2]) for r in rings]
 
 
+def run_direct(rings):
+    copies = []
+    for r in rings:
+        n = r["n"]
+        for k in range(1, n):
+            dest = lax.rem(r["me"] + k, n)
+            copy = pltpu.make_async_remote_copy(
+                src_ref=r["chunk"].at[dest],
+                dst_ref=r["recv"].at[k - 1],
+                send_sem=r["ssem"].at[r["base"] + k - 1],
+                recv_sem=r["rsem"].at[r["base"] + k - 1],
+                device_id=r["dev"](dest),
+                device_id_type=MESH,
+            )
+            copy.start()
+            copies.append(copy)
+    for copy in copies:
+        copy.wait()
+
+
 def rs_kernel(ny, nz, xa, xb, oa, ob, s1a, s1b, *bufs):
     ssem, rsem = bufs[-2:]
     bufs = bufs[:-2]
@@ -93,9 +113,11 @@
     y_left = dev(lax.rem(y + ny - 1, ny), z)
 
     barrier = pltpu.get_barrier_semaphore()
-    for peer in (z_right, z_left, y_right, y_left):
-        pl.semaphore_signal(barrier, inc=1, device_id=peer, device_id_type=MESH)
-    pl.semaphore_wait(barrier, 4)
+    for k in range(1, ny):
+        pl.semaphore_signal(barrier, inc=1, device_id=dev(lax.rem(y + k, ny), z), device_id_type=MESH)
+    for k in range(1, nz):
+        pl.semaphore_signal(barrier, inc=1, device_id=dev(y, lax.rem(z + k, nz)), device_id_type=MESH)
+    pl.semaphore_wait(barrier, ny + nz - 2)
 
     def ring(n, me, right, left, chunk, at, base):
         rr, rl, sr, sl = bufs[4 * at: 4 * at + 4]
@@ -108,12 +130,15 @@
     ])
     s1a[...] = xa[z] + ar[...] + al[...]
     s1b[...] = xb[y] + br[...] + bl[...]
-    (ar, al), (br, bl) = run_rings([
-        ring(ny, y, y_right, y_left, s1a, 2, nz + ny - 2),
-        ring(nz, z, z_right, z_left, s1b, 3, nz + 2 * ny - 3),
+    recv_a, recv_b = bufs[8], bufs[9]
+    run_direct([
+        dict(n=ny, me=y, dev=lambda d: dev(d, z), chunk=s1a, recv=recv_a,
+             ssem=ssem, rsem=rsem, base=nz + ny - 2),
+        dict(n=nz, me=z, dev=lambda d: dev(y, d), chunk=s1b, recv=recv_b,
+             ssem=ssem, rsem=rsem, base=nz + 2 * ny - 3),
     ])
-    oa[...] = s1a[y] + ar[...] + al[...]
-    ob[...] = s1b[z] + br[...] + bl[...]
+    oa[...] = s1a[y] + jnp.sum(recv_a[...], axis=0)
+    ob[...] = s1b[z] + jnp.sum(recv_b[...], axis=0)
 
 
 def reduce_scatter(xa, xb, ny, nz):
@@ -125,7 +150,7 @@
 
     bufs = (
         slots(nz, (ny, ra, LANES)) + slots(ny, (nz, rb, LANES))
-        + slots(ny, (ra, LANES)) + slots(nz, (rb, LANES))
+        + [pltpu.VMEM((ny - 1, ra, LANES), f32), pltpu.VMEM((nz - 1, rb, LANES), f32)]
     )
     return pl.pallas_call(
         functools.partial(rs_kernel, ny, nz),

time: 65.9 us -> 59.9 us (0.909)
  Pallas kernels: 51.4 us -> 45.4 us
    pallas_call x1, Pallas kernels: 44.1 us -> 38.1 us  [reduce_scatter(): pl.pallas_call(functools.partial(rs_kernel, ny, nz), out_shape=(jax.Shape...]
where the time goes in v6:
time: 59.9 us; the launch traced here: 59.6 us
  Pallas kernels  45.4 us (76%)
  matrix products  6.67 us (11%)
  other arithmetic  5.43 us (9%)
  local copies, waits for them, and re-layouts  1.93 us (3%)
    pallas_call x1, Pallas kernels, reduce_scatter(): pl.pallas_call(functools.partial(rs_kernel, ny, nz), out_shape=(jax.Shape...  38.1 us
    pallas_call x1, Pallas kernels, owner_sums(): pl.pallas_call(sums_kernel, out_shape=jax.ShapeDtypeStruct((proj.shape[1]...  7.31 us
    dot_general x1, matrix products, invert_block(): jnp.dot(scaled, table.T, precision=lax.Precision.HIGH, preferred_element_...  2.59 us
    another operation x1, other arithmetic  2.48 us
    dot_general x1, matrix products, per_device(): jnp.einsum('yzbmc,pyzmcl->pyzbl', choose[:, :, half:], parts, preferred_e...  2.43 us
    dot_general x1, matrix products, per_device(): jnp.einsum('yzbmc,pyzmcl->pzybl', choose[:, :, :half], parts, preferred_e...  1.65 us

profile of v6, /device:TPU:6, one launch (start us, length us, event | category | flops | bytes accessed | tf_op | source)
XLA Modules:
  0.0 59.6 jit_solution(4749391024745758328)
XLA Ops:
  0.0 0.7 %constant_dynamic-slice_fusion.2 = (s32[1,512]{1,0:T(1,128)S(1)}, s32[1,512]{1,0:T(1,128)S(1)}) fusion(s32[8,512]{1,0:T(8,128)} %param.7, s32[]{:T(128)S(6)} %select_n.68, s32[8,512]{1,0:T(8,128)} %param.6), kind=kLoop, calls=%fused_computation.65 | loop fusion | bytes 8196 | tf_op jit(solution)/shard_map/jit(dynamic_index_in_dim)/dynamic_slice | solution.py:206
  0.7 0.2 select_reduce_fusion
  1.0 0.1 reshape.238
  1.1 0.2 reduce_window_sum.11
  1.4 0.1 copy.20
  1.4 0.1 copy.23
  1.5 0.1 compare_and_fusion
  1.6 0.1 copy.17
  1.6 0.1 add_minimum_fusion
  1.7 0.1 min.52
  1.8 0.1 convert_reduce_fusion
  1.9 0.1 select_reduce_fusion.1
  2.0 0.1 copy.21
  2.1 0.1 copy.24
  2.3 1.0 %fusion.12.perm_ref = bf16[512,512]{1,0:T(8,128)(2,1)} fusion(s32[512]{0:T(512)S(1)} %bitcast.43), kind=kLoop, calls=%fused_computation.25 | loop fusion | flops 524288 | bytes 526336 | tf_op jit(solution)/shard_map/convert_element_type | solution.py:210
  3.3 0.4 convert_convert_fusion
  3.7 7.3 %shard_map.46 = f32[512,1024]{1,0:T(8,128)} custom-call(bf16[512,512]{1,0:T(8,128)(2,1)} %fusion.12.perm_ref, bf16[12,512,128]{2,1,0:T(8,128)(2,1)} %proj_ref.1, bf16[6,256,1024]{2,1,0:T(8,128)(2,1)} %tiles_ref.1), custom_call_target="tpu_custom_call" | custom-call | tf_op jit(solution)/shard_map/pallas_call | solution.py:187
  11.0 2.5 %reduce-precision_convert_fusion.1 = (bf16[1,8,8,8,8,128]{5,3,4,0,1,2:T(8,128)(2,1)S(1)}, bf16[1,8,8,8,8,128]{5,3,4,0,1,2:T(8,128)(2,1)S(1)}, bf16[1,8,8,8,8,128]{5,3,4,0,1,2:T(8,128)(2,1)S(1)}) fusion(f32[1,8,8,8,8,128]{5,3,4,2,1,0:T(8,128)} %bitcast.38), kind=kLoop, calls=%fused_computation.9 | loop fusion | flops 3670016 | bytes 5242880 | tf_op jit(solution)/shard_map/convert
  13.5 1.6 %bitcast_reduce_fusion.1 = f32[8,8,128,22]{2,3,1,0:T(8,128)} fusion(bf16[8,8,43,8,8]{2,3,4,0,1:T(8,128)(2,1)S(1)} %convert_convert_fusion, bf16[1,8,8,8,8,128]{5,3,4,0,1,2:T(8,128)(2,1)S(1)} %get-tuple-element.10, bf16[1,8,8,8,8,128]{5,3,4,0,1,2:T(8,128)(2,1)S(1)} %get-tuple-element.11, bf16[1,8,8,8,8,128]{5,3,4,0,1,2:T(8,128)(2,1)S(1)} %get-tuple-element.9), kind=kOutput, calls=%fused_computation.11 | convolution fusion | flops 72712192 | bytes 4218880 | tf_op jit(solution)/shard_map/yzbmc,pyzmcl->pzybl/dot_general | solution.py:236
  15.1 2.4 %bitcast_reduce_fusion = f32[8,8,128,21]{2,3,1,0:T(8,128)} fusion(bf16[1,8,8,8,8,128]{5,3,4,0,1,2:T(8,128)(2,1)S(1)} %get-tuple-element.10, bf16[1,8,8,8,8,128]{5,3,4,0,1,2:T(8,128)(2,1)S(1)} %get-tuple-element.11, bf16[1,8,8,8,8,128]{5,3,4,0,1,2:T(8,128)(2,1)S(1)} %get-tuple-element.9, bf16[8,8,43,8,8]{2,3,4,0,1:T(8,128)(2,1)S(1)} %convert_convert_fusion), kind=kOutput, calls=%fused_computation.10 | convolution fusion | flops 69550080 | bytes 4186112 | tf_op jit(solution)/shard_map/yzbmc,pyzmcl->pyzbl/dot_general | solution.py:238
  17.5 38.1 %shard_map.47 = (f32[22,128]{1,0:T(8,128)}, f32[21,128]{1,0:T(8,128)}) custom-call(f32[8,8,22,128]{3,2,1,0:T(8,128)} %bitcast.39, f32[8,8,21,128]{3,2,1,0:T(8,128)} %bitcast.40), custom_call_target="tpu_custom_call" | custom-call | tf_op jit(solution)/shard_map/pallas_call | solution.py:155
  55.6 0.7 %pad_maximum_fusion.1 = f32[43,128]{1,0:T(8,128)S(1)} fusion(f32[21,128]{1,0:T(8,128)} %get-tuple-element.8, f32[22,128]{1,0:T(8,128)} %get-tuple-element.7), kind=kLoop, calls=%fused_computation.49 | loop fusion | flops 5504 | bytes 44032 | tf_op jit(solution)/shard_map/concatenate | solution.py:241
  56.4 0.6 %gather_fusion = f32[64,128]{1,0:T(8,128)S(1)} fusion(f32[43,128]{1,0:T(8,128)S(1)} %pad_maximum_fusion.1, s32[1024]{0:T(1024)S(1)} %pad_clamp_fusion), kind=kCustom, calls=%fused_computation | custom fusion | bytes 65792 | tf_op jit(solution)/shard_map/jit(_take)/gather | solution.py:247
  57.0 2.6 %fusion.10 = f32[1,8,1024]{2,1,0:T(8,128)} fusion(f32[8,1024]{1,0:T(8,128)S(1)} %gather.7, f32[1024]{0:T(1024)S(1)} %iota_add_fusion, f32[8]{0:T(128)S(1)} %fusion.30, pred[8,8]{0,1:T(8,128)(4,1)S(1)} %copy.17), kind=kOutput, calls=%fused_computation.18 | convolution fusion | flops 53592064 | bytes 69728 | tf_op jit(solution)/shard_map/dot_general | solution.py:33
  (14 shorter events, 0.2 us)

commit v7 on v6

--- a/solution.py
+++ b/solution.py
@@ -42,37 +42,38 @@
 
 
 def run_rings(rings):
-    copies_at = []
-    for s in range(max(r["n"] // 2 for r in rings)):
-        copies = []
-        for r in rings:
+    chains = []
+    for r in rings:
+        n = r["n"]
+        nr = n // 2
+        nl = n - 1 - nr
+        chains.append((r, 1, nr, r["right"], r["rr"], r["sr"], r["base"]))
+        chains.append((r, -1, nl, r["left"], r["rl"], r["sl"], r["base"] + nr))
+    pending = [None] * len(chains)
+    for s in range(max(c[2] for c in chains)):
+        for i, (r, go, steps, to, recv, send, base) in enumerate(chains):
+            if s >= steps:
+                continue
             n = r["n"]
-            nr = n // 2
-            nl = n - 1 - nr
-            for go, steps, to, recv, send, sem in (
-                (1, nr, r["right"], r["rr"], r["sr"], r["base"] + s),
-                (-1, nl, r["left"], r["rl"], r["sl"], r["base"] + nr + s),
-            ):
-                if s >= steps:
-                    continue
-                dest = lax.rem(r["me"] + go * (steps - s) + 2 * n, n)
-                if s == 0:
-                    src = r["chunk"].at[dest]
-                else:
-                    send[s] = recv[s - 1] + r["chunk"][dest]
-                    src = send.at[s]
-                copy = pltpu.make_async_remote_copy(
-                    src_ref=src,
-                    dst_ref=recv.at[s],
-                    send_sem=r["ssem"].at[sem],
-                    recv_sem=r["rsem"].at[sem],
-                    device_id=to,
-                    device_id_type=MESH,
-                )
-                copy.start()
-                copies.append(copy)
-        for copy in copies:
-            copy.wait()
+            dest = lax.rem(r["me"] + go * (steps - s) + 2 * n, n)
+            if s == 0:
+                src = r["src"](dest)
+            else:
+                pending[i].wait()
+                send[s] = recv[s - 1] + r["val"](dest)
+                src = send.at[s]
+            copy = pltpu.make_async_remote_copy(
+                src_ref=src,
+                dst_ref=recv.at[s],
+                send_sem=r["ssem"].at[base + s],
+                recv_sem=r["rsem"].at[base + s],
+                device_id=to,
+                device_id_type=MESH,
+            )
+            copy.start()
+            pending[i] = copy
+    for copy in pending:
+        copy.wait()
     return [(r["rr"].at[r["n"] // 2 - 1], r["rl"].at[r["n"] - 2 - r["n"] // 2]) for r in rings]
 
 
@@ -119,23 +120,31 @@
         pl.semaphore_signal(barrier, inc=1, device_id=dev(y, lax.rem(z + k, nz)), device_id_type=MESH)
     pl.semaphore_wait(barrier, ny + nz - 2)
 
-    def ring(n, me, right, left, chunk, at, base):
+    def ring(n, me, right, left, x, part, at, base):
         rr, rl, sr, sl = bufs[4 * at: 4 * at + 4]
-        return dict(n=n, me=me, right=right, left=left, chunk=chunk, rr=rr, rl=rl, sr=sr, sl=sl,
+        return dict(n=n, me=me, right=right, left=left, rr=rr, rl=rl, sr=sr, sl=sl,
+                    src=lambda d: x.at[d, part], val=lambda d: x[d, part],
                     ssem=ssem, rsem=rsem, base=base)
 
-    (ar, al), (br, bl) = run_rings([
-        ring(nz, z, z_right, z_left, xa, 0, 0),
-        ring(ny, y, y_right, y_left, xb, 1, nz - 1),
+    ha, hb = ny // 2, nz // 2
+    lo_a, hi_a = pl.ds(0, ha), pl.ds(ha, ny - ha)
+    lo_b, hi_b = pl.ds(0, hb), pl.ds(hb, nz - hb)
+    fins = run_rings([
+        ring(nz, z, z_right, z_left, xa, lo_a, 0, 0),
+        ring(nz, z, z_right, z_left, xa, hi_a, 1, nz - 1),
+        ring(ny, y, y_right, y_left, xb, lo_b, 2, 2 * (nz - 1)),
+        ring(ny, y, y_right, y_left, xb, hi_b, 3, 2 * (nz - 1) + ny - 1),
     ])
-    s1a[...] = xa[z] + ar[...] + al[...]
-    s1b[...] = xb[y] + br[...] + bl[...]
-    recv_a, recv_b = bufs[8], bufs[9]
+    s1a[lo_a] = xa[z, lo_a] + fins[0][0][...] + fins[0][1][...]
+    s1a[hi_a] = xa[z, hi_a] + fins[1][0][...] + fins[1][1][...]
+    s1b[lo_b] = xb[y, lo_b] + fins[2][0][...] + fins[2][1][...]
+    s1b[hi_b] = xb[y, hi_b] + fins[3][0][...] + fins[3][1][...]
+    recv_a, recv_b = bufs[16], bufs[17]
     run_direct([
         dict(n=ny, me=y, dev=lambda d: dev(d, z), chunk=s1a, recv=recv_a,
-             ssem=ssem, rsem=rsem, base=nz + ny - 2),
+             ssem=ssem, rsem=rsem, base=2 * (nz + ny - 2)),
         dict(n=nz, me=z, dev=lambda d: dev(y, d), chunk=s1b, recv=recv_b,
-             ssem=ssem, rsem=rsem, base=nz + 2 * ny - 3),
+             ssem=ssem, rsem=rsem, base=2 * (nz + ny - 2) + ny - 1),
     ])
     oa[...] = s1a[y] + jnp.sum(recv_a[...], axis=0)
     ob[...] = s1b[z] + jnp.sum(recv_b[...], axis=0)
@@ -148,8 +157,10 @@
     def slots(n, shape):
         return [pltpu.VMEM((n // 2,) + shape, f32), pltpu.VMEM((n - 1 - n // 2,) + shape, f32)] * 2
 
+    ha, hb = ny // 2, nz // 2
     bufs = (
-        slots(nz, (ny, ra, LANES)) + slots(ny, (nz, rb, LANES))
+        slots(nz, (ha, ra, LANES)) + slots(nz, (ny - ha, ra, LANES))
+        + slots(ny, (hb, rb, LANES)) + slots(ny, (nz - hb, rb, LANES))
         + [pltpu.VMEM((ny - 1, ra, LANES), f32), pltpu.VMEM((nz - 1, rb, LANES), f32)]
     )
     return pl.pallas_call(
@@ -159,7 +170,7 @@
         out_specs=(pl.BlockSpec(memory_space=pltpu.VMEM),) * 2,
         scratch_shapes=[pltpu.VMEM((ny, ra, LANES), f32), pltpu.VMEM((nz, rb, LANES), f32)]
         + bufs
-        + [pltpu.SemaphoreType.DMA((2 * (nz + ny - 2),)), pltpu.SemaphoreType.DMA((2 * (nz + ny - 2),))],
+        + [pltpu.SemaphoreType.DMA((3 * (nz + ny - 2),)), pltpu.SemaphoreType.DMA((3 * (nz + ny - 2),))],
         compiler_params=pltpu.CompilerParams(collective_id=0, has_side_effects=True),
     )(xa, xb)
 

time: 59.9 us -> 59.3 us (0.990)
  Pallas kernels: 45.4 us -> 44.7 us
    pallas_call x1, Pallas kernels: 38.1 us -> 37.4 us  [reduce_scatter(): pl.pallas_call(functools.partial(rs_kernel, ny, nz), out_shape=(jax.Shape...]
where the time goes in v7:
time: 59.3 us; the launch traced here: 58.9 us
  Pallas kernels  44.7 us (75%)
  matrix products  6.67 us (11%)
  other arithmetic  5.43 us (9%)
  local copies, waits for them, and re-layouts  1.93 us (3%)
    pallas_call x1, Pallas kernels, reduce_scatter(): pl.pallas_call(functools.partial(rs_kernel, ny, nz), out_shape=(jax.Shape...  37.4 us
    pallas_call x1, Pallas kernels, owner_sums(): pl.pallas_call(sums_kernel, out_shape=jax.ShapeDtypeStruct((proj.shape[1]...  7.31 us
    dot_general x1, matrix products, invert_block(): jnp.dot(scaled, table.T, precision=lax.Precision.HIGH, preferred_element_...  2.59 us
    another operation x1, other arithmetic  2.48 us
    dot_general x1, matrix products, per_device(): jnp.einsum('yzbmc,pyzmcl->pyzbl', choose[:, :, half:], parts, preferred_e...  2.43 us
    dot_general x1, matrix products, per_device(): jnp.einsum('yzbmc,pyzmcl->pzybl', choose[:, :, :half], parts, preferred_e...  1.65 us

profile of v7, /device:TPU:6, one launch (start us, length us, event | category | flops | bytes accessed | tf_op | source)
XLA Modules:
  0.0 58.9 jit_solution(9131905041321165309)
XLA Ops:
  0.0 0.7 %constant_dynamic-slice_fusion.2 = (s32[1,512]{1,0:T(1,128)S(1)}, s32[1,512]{1,0:T(1,128)S(1)}) fusion(s32[8,512]{1,0:T(8,128)} %param.7, s32[]{:T(128)S(6)} %select_n.68, s32[8,512]{1,0:T(8,128)} %param.6), kind=kLoop, calls=%fused_computation.65 | loop fusion | bytes 8196 | tf_op jit(solution)/shard_map/jit(dynamic_index_in_dim)/dynamic_slice | solution.py:217
  0.7 0.2 select_reduce_fusion
  1.0 0.1 reshape.238
  1.1 0.2 reduce_window_sum.11
  1.4 0.1 copy.20
  1.4 0.1 copy.23
  1.5 0.1 compare_and_fusion
  1.6 0.1 copy.17
  1.6 0.1 add_minimum_fusion
  1.7 0.1 min.52
  1.8 0.1 convert_reduce_fusion
  1.9 0.1 select_reduce_fusion.1
  2.0 0.1 copy.21
  2.1 0.1 copy.24
  2.3 1.0 %fusion.12.perm_ref = bf16[512,512]{1,0:T(8,128)(2,1)} fusion(s32[512]{0:T(512)S(1)} %bitcast.43), kind=kLoop, calls=%fused_computation.25 | loop fusion | flops 524288 | bytes 526336 | tf_op jit(solution)/shard_map/convert_element_type | solution.py:221
  3.3 0.4 convert_convert_fusion
  3.7 7.3 %shard_map.46 = f32[512,1024]{1,0:T(8,128)} custom-call(bf16[512,512]{1,0:T(8,128)(2,1)} %fusion.12.perm_ref, bf16[12,512,128]{2,1,0:T(8,128)(2,1)} %proj_ref.1, bf16[6,256,1024]{2,1,0:T(8,128)(2,1)} %tiles_ref.1), custom_call_target="tpu_custom_call" | custom-call | tf_op jit(solution)/shard_map/pallas_call | solution.py:198
  11.0 2.5 %reduce-precision_convert_fusion.1 = (bf16[1,8,8,8,8,128]{5,3,4,0,1,2:T(8,128)(2,1)S(1)}, bf16[1,8,8,8,8,128]{5,3,4,0,1,2:T(8,128)(2,1)S(1)}, bf16[1,8,8,8,8,128]{5,3,4,0,1,2:T(8,128)(2,1)S(1)}) fusion(f32[1,8,8,8,8,128]{5,3,4,2,1,0:T(8,128)} %bitcast.38), kind=kLoop, calls=%fused_computation.9 | loop fusion | flops 3670016 | bytes 5242880 | tf_op jit(solution)/shard_map/convert
  13.5 1.6 %bitcast_reduce_fusion.1 = f32[8,8,128,22]{2,3,1,0:T(8,128)} fusion(bf16[8,8,43,8,8]{2,3,4,0,1:T(8,128)(2,1)S(1)} %convert_convert_fusion, bf16[1,8,8,8,8,128]{5,3,4,0,1,2:T(8,128)(2,1)S(1)} %get-tuple-element.10, bf16[1,8,8,8,8,128]{5,3,4,0,1,2:T(8,128)(2,1)S(1)} %get-tuple-element.11, bf16[1,8,8,8,8,128]{5,3,4,0,1,2:T(8,128)(2,1)S(1)} %get-tuple-element.9), kind=kOutput, calls=%fused_computation.11 | convolution fusion | flops 72712192 | bytes 4218880 | tf_op jit(solution)/shard_map/yzbmc,pyzmcl->pzybl/dot_general | solution.py:247
  15.1 2.4 %bitcast_reduce_fusion = f32[8,8,128,21]{2,3,1,0:T(8,128)} fusion(bf16[1,8,8,8,8,128]{5,3,4,0,1,2:T(8,128)(2,1)S(1)} %get-tuple-element.10, bf16[1,8,8,8,8,128]{5,3,4,0,1,2:T(8,128)(2,1)S(1)} %get-tuple-element.11, bf16[1,8,8,8,8,128]{5,3,4,0,1,2:T(8,128)(2,1)S(1)} %get-tuple-element.9, bf16[8,8,43,8,8]{2,3,4,0,1:T(8,128)(2,1)S(1)} %convert_convert_fusion), kind=kOutput, calls=%fused_computation.10 | convolution fusion | flops 69550080 | bytes 4186112 | tf_op jit(solution)/shard_map/yzbmc,pyzmcl->pyzbl/dot_general | solution.py:249
  17.5 37.4 %shard_map.47 = (f32[22,128]{1,0:T(8,128)}, f32[21,128]{1,0:T(8,128)}) custom-call(f32[8,8,22,128]{3,2,1,0:T(8,128)} %bitcast.39, f32[8,8,21,128]{3,2,1,0:T(8,128)} %bitcast.40), custom_call_target="tpu_custom_call" | custom-call | tf_op jit(solution)/shard_map/pallas_call | solution.py:166
  55.0 0.7 %pad_maximum_fusion.1 = f32[43,128]{1,0:T(8,128)S(1)} fusion(f32[21,128]{1,0:T(8,128)} %get-tuple-element.8, f32[22,128]{1,0:T(8,128)} %get-tuple-element.7), kind=kLoop, calls=%fused_computation.49 | loop fusion | flops 5504 | bytes 44032 | tf_op jit(solution)/shard_map/concatenate | solution.py:252
  55.7 0.6 %gather_fusion = f32[64,128]{1,0:T(8,128)S(1)} fusion(f32[43,128]{1,0:T(8,128)S(1)} %pad_maximum_fusion.1, s32[1024]{0:T(1024)S(1)} %pad_clamp_fusion), kind=kCustom, calls=%fused_computation | custom fusion | bytes 65792 | tf_op jit(solution)/shard_map/jit(_take)/gather | solution.py:258
  56.3 2.6 %fusion.10 = f32[1,8,1024]{2,1,0:T(8,128)} fusion(f32[8,1024]{1,0:T(8,128)S(1)} %gather.7, f32[1024]{0:T(1024)S(1)} %iota_add_fusion, f32[8]{0:T(128)S(1)} %fusion.30, pred[8,8]{0,1:T(8,128)(4,1)S(1)} %copy.17), kind=kOutput, calls=%fused_computation.18 | convolution fusion | flops 53592064 | bytes 69728 | tf_op jit(solution)/shard_map/dot_general | solution.py:33
  (14 shorter events, 0.2 us)

commit v8 on v7

--- a/solution.py
+++ b/solution.py
@@ -175,32 +175,25 @@
     )(xa, xb)
 
 
-def sums_kernel(perm_ref, proj_ref, tiles_ref, out_ref):
+def sums_kernel(proj_ref, tiles_ref, out_ref):
     blocks, pair, samples = tiles_ref.shape
     footprint = proj_ref.shape[2]
     per = pair // footprint
-    perm = perm_ref[...]
     total = None
     for b in range(blocks):
-        lhs = jnp.concatenate(
-            [
-                jnp.dot(perm, proj_ref[b * per + h], preferred_element_type=jnp.float32)
-                for h in range(per)
-            ],
-            axis=1,
-        ).astype(proj_ref.dtype)
+        lhs = jnp.concatenate([proj_ref[b * per + h] for h in range(per)], axis=1)
         term = jnp.dot(lhs, tiles_ref[b], preferred_element_type=jnp.float32)
         total = term if total is None else total + term
     out_ref[...] = total
 
 
-def owner_sums(perm, proj, tiles):
+def owner_sums(proj, tiles):
     return pl.pallas_call(
         sums_kernel,
         out_shape=jax.ShapeDtypeStruct((proj.shape[1], tiles.shape[2]), jnp.float32),
-        in_specs=[pl.BlockSpec(memory_space=pltpu.VMEM)] * 3,
+        in_specs=[pl.BlockSpec(memory_space=pltpu.VMEM)] * 2,
         out_specs=pl.BlockSpec(memory_space=pltpu.VMEM),
-    )(perm, proj, tiles)
+    )(proj, tiles)
 
 
 def per_device(ny, nz, proj, tiles, owner, lengths):
@@ -219,7 +212,8 @@
     order_len = order_len.reshape(view_devices, owned)
 
     perm = (my_order[:, None] == jnp.arange(group_rows, dtype=jnp.int32)[None, :]).astype(proj.dtype)
-    sums = owner_sums(perm, proj, tiles)
+    proj_ord = jnp.einsum("rk,vkd->vrd", perm, proj, preferred_element_type=jnp.float32)
+    sums = owner_sums(proj_ord.astype(proj.dtype), tiles)
     blocks = sums.reshape(ny, nz, owned, chunks_per_row, LANES)
 
     counts = (order_len + LANES - 1) // LANES

time: 59.3 us -> 58.7 us (0.990)
  matrix products: 6.67 us -> 8.85 us
  Pallas kernels: 44.7 us -> 42.9 us
  other arithmetic: 5.43 us -> 4.48 us
    dot_general x0 -> x1, matrix products: none -> 2.18 us  [per_device(): jnp.einsum('rk,vkd->vrd', perm, proj, preferred_element_type=jnp.float32)]
    pallas_call x1, Pallas kernels: 7.31 us -> 5.5 us  [owner_sums(): pl.pallas_call(sums_kernel, out_shape=jax.ShapeDtypeStruct((proj.shape[1]...]
    convert_element_type x1 -> x0, other arithmetic: 0.95 us -> none  [per_device(): (my_order[:, None] == jnp.arange(group_rows, dtype=jnp.int32)[None, :]).a...]
where the time goes in v8:
time: 58.7 us; the launch traced here: 58.5 us
  Pallas kernels  42.9 us (73%)
  matrix products  8.85 us (15%)
  other arithmetic  4.48 us (8%)
  local copies, waits for them, and re-layouts  2.05 us (3%)
    pallas_call x1, Pallas kernels, reduce_scatter(): pl.pallas_call(functools.partial(rs_kernel, ny, nz), out_shape=(jax.Shape...  37.4 us
    pallas_call x1, Pallas kernels, owner_sums(): pl.pallas_call(sums_kernel, out_shape=jax.ShapeDtypeStruct((proj.shape[1]...  5.5 us
    dot_general x1, matrix products, invert_block(): jnp.dot(scaled, table.T, precision=lax.Precision.HIGH, preferred_element_...  2.59 us
    another operation x1, other arithmetic  2.48 us
    dot_general x1, matrix products, per_device(): jnp.einsum('yzbmc,pyzmcl->pyzbl', choose[:, :, half:], parts, preferred_e...  2.43 us
    dot_general x1, matrix products, per_device(): jnp.einsum('rk,vkd->vrd', perm, proj, preferred_element_type=jnp.float32)  2.18 us
    dot_general x1, matrix products, per_device(): jnp.einsum('yzbmc,pyzmcl->pzybl', choose[:, :, :half], parts, preferred_e...  1.65 us

profile of v8, /device:TPU:6, one launch (start us, length us, event | category | flops | bytes accessed | tf_op | source)
XLA Modules:
  0.0 58.5 jit_solution(17404775553416350462)
XLA Ops:
  0.0 0.0 copy-start
  0.0 0.9 %constant_dynamic-slice_fusion.2 = (s32[1,512]{1,0:T(1,128)S(1)}, s32[1,512]{1,0:T(1,128)S(1)}) fusion(s32[8,512]{1,0:T(8,128)} %param.7, s32[]{:T(128)S(6)} %select_n.68, s32[8,512]{1,0:T(8,128)} %param.6), kind=kLoop, calls=%fused_computation.68 | loop fusion | bytes 8196 | tf_op jit(solution)/shard_map/jit(dynamic_index_in_dim)/dynamic_slice | solution.py:210
  0.9 0.2 select_reduce_fusion
  1.1 0.1 reshape.238
  1.3 0.2 reduce_window_sum.11
  1.5 0.1 copy.20
  1.5 0.1 copy.23
  1.6 0.1 compare_and_fusion
  1.7 0.1 copy.17
  1.8 0.1 add_minimum_fusion
  1.8 0.1 min.52
  2.0 0.1 convert_reduce_fusion
  2.0 0.1 select_reduce_fusion.1
  2.1 0.1 copy.21
  2.2 0.1 copy.24
  2.4 0.4 convert_convert_fusion
  2.8 0.0 copy-done
  2.8 2.2 %fusion.8.proj_ref = bf16[12,512,128]{2,1,0:T(8,128)(2,1)} fusion(bf16[12,512,128]{2,1,0:T(8,128)(2,1)S(1)} %copy-done, s32[512]{0:T(512)S(1)} %bitcast.49), kind=kOutput, calls=%fused_computation.17 | convolution fusion | flops 806354944 | bytes 3147776 | tf_op jit(solution)/shard_map/rk,vkd->vrd/dot_general | solution.py:215
  5.0 5.5 %shard_map.46 = f32[512,1024]{1,0:T(8,128)} custom-call(bf16[12,512,128]{2,1,0:T(8,128)(2,1)} %fusion.8.proj_ref, bf16[6,256,1024]{2,1,0:T(8,128)(2,1)} %tiles_ref.1), custom_call_target="tpu_custom_call" | custom-call | tf_op jit(solution)/shard_map/pallas_call | solution.py:191
  10.5 2.5 %reduce-precision_convert_fusion.1 = (bf16[1,8,8,8,8,128]{5,3,4,0,1,2:T(8,128)(2,1)S(1)}, bf16[1,8,8,8,8,128]{5,3,4,0,1,2:T(8,128)(2,1)S(1)}, bf16[1,8,8,8,8,128]{5,3,4,0,1,2:T(8,128)(2,1)S(1)}) fusion(f32[1,8,8,8,8,128]{5,3,4,2,1,0:T(8,128)} %bitcast.44), kind=kLoop, calls=%fused_computation.9 | loop fusion | flops 3670016 | bytes 5242880 | tf_op jit(solution)/shard_map/convert
  13.0 1.6 %bitcast_reduce_fusion.1 = f32[8,8,128,22]{2,3,1,0:T(8,128)} fusion(bf16[8,8,43,8,8]{2,3,4,0,1:T(8,128)(2,1)S(1)} %convert_convert_fusion, bf16[1,8,8,8,8,128]{5,3,4,0,1,2:T(8,128)(2,1)S(1)} %get-tuple-element.10, bf16[1,8,8,8,8,128]{5,3,4,0,1,2:T(8,128)(2,1)S(1)} %get-tuple-element.11, bf16[1,8,8,8,8,128]{5,3,4,0,1,2:T(8,128)(2,1)S(1)} %get-tuple-element.9), kind=kOutput, calls=%fused_computation.11 | convolution fusion | flops 72712192 | bytes 4218880 | tf_op jit(solution)/shard_map/yzbmc,pyzmcl->pzybl/dot_general | solution.py:241
  14.7 2.4 %bitcast_reduce_fusion = f32[8,8,128,21]{2,3,1,0:T(8,128)} fusion(bf16[1,8,8,8,8,128]{5,3,4,0,1,2:T(8,128)(2,1)S(1)} %get-tuple-element.10, bf16[1,8,8,8,8,128]{5,3,4,0,1,2:T(8,128)(2,1)S(1)} %get-tuple-element.11, bf16[1,8,8,8,8,128]{5,3,4,0,1,2:T(8,128)(2,1)S(1)} %get-tuple-element.9, bf16[8,8,43,8,8]{2,3,4,0,1:T(8,128)(2,1)S(1)} %convert_convert_fusion), kind=kOutput, calls=%fused_computation.10 | convolution fusion | flops 69550080 | bytes 4186112 | tf_op jit(solution)/shard_map/yzbmc,pyzmcl->pyzbl/dot_general | solution.py:243
  17.1 37.4 %shard_map.47 = (f32[22,128]{1,0:T(8,128)}, f32[21,128]{1,0:T(8,128)}) custom-call(f32[8,8,22,128]{3,2,1,0:T(8,128)} %bitcast.45, f32[8,8,21,128]{3,2,1,0:T(8,128)} %bitcast.46), custom_call_target="tpu_custom_call" | custom-call | tf_op jit(solution)/shard_map/pallas_call | solution.py:166
  54.5 0.7 %pad_maximum_fusion.1 = f32[43,128]{1,0:T(8,128)S(1)} fusion(f32[21,128]{1,0:T(8,128)} %get-tuple-element.8, f32[22,128]{1,0:T(8,128)} %get-tuple-element.7), kind=kLoop, calls=%fused_computation.52 | loop fusion | flops 5504 | bytes 44032 | tf_op jit(solution)/shard_map/concatenate | solution.py:246
  55.3 0.6 %gather_fusion = f32[64,128]{1,0:T(8,128)S(1)} fusion(f32[43,128]{1,0:T(8,128)S(1)} %pad_maximum_fusion.1, s32[1024]{0:T(1024)S(1)} %pad_clamp_fusion), kind=kCustom, calls=%fused_computation | custom fusion | bytes 65792 | tf_op jit(solution)/shard_map/jit(_take)/gather | solution.py:252
  55.9 2.6 %fusion.11 = f32[1,8,1024]{2,1,0:T(8,128)} fusion(f32[8,1024]{1,0:T(8,128)S(1)} %gather.7, f32[1024]{0:T(1024)S(1)} %iota_add_fusion, f32[8]{0:T(128)S(1)} %fusion.33, pred[8,8]{0,1:T(8,128)(4,1)S(1)} %copy.17), kind=kOutput, calls=%fused_computation.20 | convolution fusion | flops 53592064 | bytes 69728 | tf_op jit(solution)/shard_map/dot_general | solution.py:33
  (14 shorter events, 0.2 us)
Async XLA Ops:
  0.0 2.8 %copy-start = (bf16[12,512,128]{2,1,0:T(8,128)(2,1)S(1)}, bf16[12,512,128]{2,1,0:T(8,128)(2,1)}, u32[]{:S(2)}) copy-start(bf16[12,512,128]{2,1,0:T(8,128)(2,1)} %param.4) | copy-start | bytes 4718596

commit v9 on v8

--- a/solution.py
+++ b/solution.py
@@ -184,13 +184,18 @@
         lhs = jnp.concatenate([proj_ref[b * per + h] for h in range(per)], axis=1)
         term = jnp.dot(lhs, tiles_ref[b], preferred_element_type=jnp.float32)
         total = term if total is None else total + term
-    out_ref[...] = total
+    hi = total.astype(jnp.bfloat16)
+    rest = total - hi.astype(jnp.float32)
+    mid = rest.astype(jnp.bfloat16)
+    out_ref[0] = hi
+    out_ref[1] = mid
+    out_ref[2] = (rest - mid.astype(jnp.float32)).astype(jnp.bfloat16)
 
 
 def owner_sums(proj, tiles):
     return pl.pallas_call(
         sums_kernel,
-        out_shape=jax.ShapeDtypeStruct((proj.shape[1], tiles.shape[2]), jnp.float32),
+        out_shape=jax.ShapeDtypeStruct((3, proj.shape[1], tiles.shape[2]), jnp.bfloat16),
         in_specs=[pl.BlockSpec(memory_space=pltpu.VMEM)] * 2,
         out_specs=pl.BlockSpec(memory_space=pltpu.VMEM),
     )(proj, tiles)
@@ -214,7 +219,7 @@
     perm = (my_order[:, None] == jnp.arange(group_rows, dtype=jnp.int32)[None, :]).astype(proj.dtype)
     proj_ord = jnp.einsum("rk,vkd->vrd", perm, proj, preferred_element_type=jnp.float32)
     sums = owner_sums(proj_ord.astype(proj.dtype), tiles)
-    blocks = sums.reshape(ny, nz, owned, chunks_per_row, LANES)
+    parts = sums.reshape(3, ny, nz, owned, chunks_per_row, LANES)
 
     counts = (order_len + LANES - 1) // LANES
     ends = jnp.cumsum(counts, axis=1)
@@ -231,13 +236,7 @@
         (member[..., None, None] == jnp.arange(owned, dtype=jnp.int32)[:, None])
         & (within[..., None, None] == jnp.arange(chunks_per_row, dtype=jnp.int32)[None, :])
     ).astype(jnp.float32)
-    bf16 = jnp.bfloat16
-    hi = lax.reduce_precision(blocks, exponent_bits=8, mantissa_bits=7)
-    rest = blocks - hi
-    mid = lax.reduce_precision(rest, exponent_bits=8, mantissa_bits=7)
-    lo = rest - mid
-    parts = jnp.stack([hi, mid, lo]).astype(bf16)
-    choose = choose.astype(bf16)
+    choose = choose.astype(jnp.bfloat16)
     xa = jnp.einsum("yzbmc,pyzmcl->pzybl", choose[:, :, :half], parts,
                     preferred_element_type=jnp.float32).sum(axis=0)
     xb = jnp.einsum("yzbmc,pyzmcl->pyzbl", choose[:, :, half:], parts,

time: 58.7 us -> 58.4 us (level)
  other arithmetic: 4.48 us -> 2 us
  matrix products: 8.85 us -> 10.5 us
    another operation x1 -> x0, other arithmetic: 2.48 us -> none
    dot_general x1, matrix products: 2.43 us -> 4.11 us  [per_device(): jnp.einsum('yzbmc,pyzmcl->pyzbl', choose[:, :, half:], parts, preferred_e...]
where the time goes in v9:
time: 58.4 us; the launch traced here: 58.1 us
  Pallas kernels  43.4 us (74%)
  matrix products  10.5 us (18%)
  local copies, waits for them, and re-layouts  2.05 us (4%)
  other arithmetic  2 us (3%)
    pallas_call x1, Pallas kernels, reduce_scatter(): pl.pallas_call(functools.partial(rs_kernel, ny, nz), out_shape=(jax.Shape...  37.4 us
    pallas_call x1, Pallas kernels, owner_sums(): pl.pallas_call(sums_kernel, out_shape=jax.ShapeDtypeStruct((3, proj.shape...  6 us
    dot_general x1, matrix products, per_device(): jnp.einsum('yzbmc,pyzmcl->pyzbl', choose[:, :, half:], parts, preferred_e...  4.11 us
    dot_general x1, matrix products, invert_block(): jnp.dot(scaled, table.T, precision=lax.Precision.HIGH, preferred_element_...  2.59 us
    dot_general x1, matrix products, per_device(): jnp.einsum('rk,vkd->vrd', perm, proj, preferred_element_type=jnp.float32)  2.17 us
    dot_general x1, matrix products, per_device(): jnp.einsum('yzbmc,pyzmcl->pzybl', choose[:, :, :half], parts, preferred_e...  1.64 us

profile of v9, /device:TPU:6, one launch (start us, length us, event | category | flops | bytes accessed | tf_op | source)
XLA Modules:
  0.0 58.1 jit_solution(10377780482191096904)
XLA Ops:
  0.0 0.0 copy-start
  0.0 0.9 %constant_dynamic-slice_fusion.2 = (s32[1,512]{1,0:T(1,128)S(1)}, s32[1,512]{1,0:T(1,128)S(1)}) fusion(s32[8,512]{1,0:T(8,128)} %param.7, s32[]{:T(128)S(6)} %select_n.68, s32[8,512]{1,0:T(8,128)} %param.6), kind=kLoop, calls=%fused_computation.64 | loop fusion | bytes 8196 | tf_op jit(solution)/shard_map/jit(dynamic_index_in_dim)/dynamic_slice | solution.py:215
  0.9 0.2 select_reduce_fusion
  1.1 0.1 reshape.202
  1.3 0.2 reduce_window_sum.11
  1.5 0.1 copy.16
  1.5 0.1 copy.19
  1.6 0.1 compare_and_fusion
  1.7 0.1 copy.15
  1.8 0.1 add_minimum_fusion
  1.8 0.1 min.52
  2.0 0.1 convert_reduce_fusion
  2.0 0.1 select_reduce_fusion.1
  2.1 0.1 copy.17
  2.2 0.1 copy.20
  2.4 0.4 convert_convert_fusion
  2.8 0.0 copy-done
  2.8 2.2 %fusion.11.proj_ref = bf16[12,512,128]{2,1,0:T(8,128)(2,1)} fusion(bf16[12,512,128]{2,1,0:T(8,128)(2,1)S(1)} %copy-done, s32[512]{0:T(512)S(1)} %bitcast.50), kind=kOutput, calls=%fused_computation.13 | convolution fusion | flops 806354944 | bytes 3147776 | tf_op jit(solution)/shard_map/rk,vkd->vrd/dot_general | solution.py:220
  5.0 6.0 %shard_map.46 = bf16[3,512,1024]{2,1,0:T(8,128)(2,1)} custom-call(bf16[12,512,128]{2,1,0:T(8,128)(2,1)} %fusion.11.proj_ref, bf16[6,256,1024]{2,1,0:T(8,128)(2,1)} %tiles_ref.1), custom_call_target="tpu_custom_call" | custom-call | tf_op jit(solution)/shard_map/pallas_call | solution.py:196
  11.0 0.0 copy-start.1
  11.0 4.1 %bitcast_reduce_fusion = f32[8,8,128,21]{2,3,1,0:T(8,128)} fusion(bf16[3,8,8,8,8,128]{5,3,4,2,1,0:T(8,128)(2,1)} %bitcast.44, bf16[8,8,43,8,8]{2,3,4,0,1:T(8,128)(2,1)S(1)} %convert_convert_fusion), kind=kOutput, calls=%fused_computation.7 | convolution fusion | flops 66404352 | bytes 4186112 | tf_op jit(solution)/shard_map/yzbmc,pyzmcl->pyzbl/dot_general | solution.py:242
  15.1 0.0 copy-done.1
  15.1 1.6 %bitcast_reduce_fusion.1 = f32[8,8,128,22]{2,3,1,0:T(8,128)} fusion(bf16[3,8,8,8,8,128]{5,3,4,2,1,0:T(8,128)(2,1)S(1)} %bitcast.45, bf16[8,8,43,8,8]{2,3,4,0,1:T(8,128)(2,1)S(1)} %convert_convert_fusion), kind=kOutput, calls=%fused_computation.8 | convolution fusion | flops 69566464 | bytes 4218880 | tf_op jit(solution)/shard_map/yzbmc,pyzmcl->pzybl/dot_general | solution.py:240
  16.8 37.4 %shard_map.47 = (f32[22,128]{1,0:T(8,128)}, f32[21,128]{1,0:T(8,128)}) custom-call(f32[8,8,22,128]{3,2,1,0:T(8,128)} %bitcast.47, f32[8,8,21,128]{3,2,1,0:T(8,128)} %bitcast.46), custom_call_target="tpu_custom_call" | custom-call | tf_op jit(solution)/shard_map/pallas_call | solution.py:166
  54.2 0.7 %pad_maximum_fusion = f32[43,128]{1,0:T(8,128)S(1)} fusion(f32[21,128]{1,0:T(8,128)} %get-tuple-element.8, f32[22,128]{1,0:T(8,128)} %get-tuple-element.7), kind=kLoop, calls=%fused_computation.48 | loop fusion | flops 5504 | bytes 44032 | tf_op jit(solution)/shard_map/concatenate | solution.py:245
  54.9 0.6 %gather_fusion = f32[64,128]{1,0:T(8,128)S(1)} fusion(f32[43,128]{1,0:T(8,128)S(1)} %pad_maximum_fusion, s32[1024]{0:T(1024)S(1)} %pad_clamp_fusion), kind=kCustom, calls=%fused_computation | custom fusion | bytes 65792 | tf_op jit(solution)/shard_map/jit(_take)/gather | solution.py:251
  55.5 2.6 %fusion.14 = f32[1,8,1024]{2,1,0:T(8,128)} fusion(f32[8,1024]{1,0:T(8,128)S(1)} %gather.7, f32[1024]{0:T(1024)S(1)} %iota_add_fusion, f32[8]{0:T(128)S(1)} %fusion.36, pred[8,8]{0,1:T(8,128)(4,1)S(1)} %copy.15), kind=kOutput, calls=%fused_computation.16 | convolution fusion | flops 53592064 | bytes 69728 | tf_op jit(solution)/shard_map/dot_general | solution.py:33
  (14 shorter events, 0.2 us)
Async XLA Ops:
  0.0 2.8 %copy-start = (bf16[12,512,128]{2,1,0:T(8,128)(2,1)S(1)}, bf16[12,512,128]{2,1,0:T(8,128)(2,1)}, u32[]{:S(2)}) copy-start(bf16[12,512,128]{2,1,0:T(8,128)(2,1)} %param.4) | copy-start | bytes 4718596
  11.0 4.1 %copy-start.1 = (bf16[3,512,1024]{2,1,0:T(8,128)(2,1)S(1)}, bf16[3,512,1024]{2,1,0:T(8,128)(2,1)}, u32[]{:S(2)}) copy-start(bf16[3,512,1024]{2,1,0:T(8,128)(2,1)} %shard_map.46) | copy-start | bytes 9437188

commit v10 on v9

--- a/solution.py
+++ b/solution.py
@@ -120,23 +120,26 @@
         pl.semaphore_signal(barrier, inc=1, device_id=dev(y, lax.rem(z + k, nz)), device_id_type=MESH)
     pl.semaphore_wait(barrier, ny + nz - 2)
 
-    def ring(n, me, right, left, x, part, at, base):
+    def ring(n, me, right, left, x, part, at, base, swap=False):
         rr, rl, sr, sl = bufs[4 * at: 4 * at + 4]
+        if swap:
+            src, val = (lambda d: x.at[part, d]), (lambda d: x[part, d])
+        else:
+            src, val = (lambda d: x.at[d, part]), (lambda d: x[d, part])
         return dict(n=n, me=me, right=right, left=left, rr=rr, rl=rl, sr=sr, sl=sl,
-                    src=lambda d: x.at[d, part], val=lambda d: x[d, part],
-                    ssem=ssem, rsem=rsem, base=base)
+                    src=src, val=val, ssem=ssem, rsem=rsem, base=base)
 
     ha, hb = ny // 2, nz // 2
     lo_a, hi_a = pl.ds(0, ha), pl.ds(ha, ny - ha)
     lo_b, hi_b = pl.ds(0, hb), pl.ds(hb, nz - hb)
     fins = run_rings([
-        ring(nz, z, z_right, z_left, xa, lo_a, 0, 0),
-        ring(nz, z, z_right, z_left, xa, hi_a, 1, nz - 1),
+        ring(nz, z, z_right, z_left, xa, lo_a, 0, 0, swap=True),
+        ring(nz, z, z_right, z_left, xa, hi_a, 1, nz - 1, swap=True),
         ring(ny, y, y_right, y_left, xb, lo_b, 2, 2 * (nz - 1)),
         ring(ny, y, y_right, y_left, xb, hi_b, 3, 2 * (nz - 1) + ny - 1),
     ])
-    s1a[lo_a] = xa[z, lo_a] + fins[0][0][...] + fins[0][1][...]
-    s1a[hi_a] = xa[z, hi_a] + fins[1][0][...] + fins[1][1][...]
+    s1a[lo_a] = xa[lo_a, z] + fins[0][0][...] + fins[0][1][...]
+    s1a[hi_a] = xa[hi_a, z] + fins[1][0][...] + fins[1][1][...]
     s1b[lo_b] = xb[y, lo_b] + fins[2][0][...] + fins[2][1][...]
     s1b[hi_b] = xb[y, hi_b] + fins[3][0][...] + fins[3][1][...]
     recv_a, recv_b = bufs[16], bufs[17]
@@ -237,7 +240,7 @@
         & (within[..., None, None] == jnp.arange(chunks_per_row, dtype=jnp.int32)[None, :])
     ).astype(jnp.float32)
     choose = choose.astype(jnp.bfloat16)
-    xa = jnp.einsum("yzbmc,pyzmcl->pzybl", choose[:, :, :half], parts,
+    xa = jnp.einsum("yzbmc,pyzmcl->pyzbl", choose[:, :, :half], parts,
                     preferred_element_type=jnp.float32).sum(axis=0)
     xb = jnp.einsum("yzbmc,pyzmcl->pyzbl", choose[:, :, half:], parts,
                     preferred_element_type=jnp.float32).sum(axis=0)

time: 58.4 us -> 58.4 us (level)
  no operation moved by 1% of the time
where the time goes in v10:
time: 58.4 us; the launch traced here: 58.1 us
  Pallas kernels  43.4 us (74%)
  matrix products  10.5 us (18%)
  local copies, waits for them, and re-layouts  2.03 us (3%)
  other arithmetic  2 us (3%)
    pallas_call x1, Pallas kernels, reduce_scatter(): pl.pallas_call(functools.partial(rs_kernel, ny, nz), out_shape=(jax.Shape...  37.4 us
    pallas_call x1, Pallas kernels, owner_sums(): pl.pallas_call(sums_kernel, out_shape=jax.ShapeDtypeStruct((3, proj.shape...  6 us
    dot_general x1, matrix products, per_device(): jnp.einsum('yzbmc,pyzmcl->pyzbl', choose[:, :, half:], parts, preferred_e...  4.11 us
    dot_general x1, matrix products, invert_block(): jnp.dot(scaled, table.T, precision=lax.Precision.HIGH, preferred_element_...  2.59 us
    dot_general x1, matrix products, per_device(): jnp.einsum('rk,vkd->vrd', perm, proj, preferred_element_type=jnp.float32)  2.17 us
    dot_general x1, matrix products, per_device(): jnp.einsum('yzbmc,pyzmcl->pyzbl', choose[:, :, :half], parts, preferred_e...  1.64 us

profile of v10, /device:TPU:6, one launch (start us, length us, event | category | flops | bytes accessed | tf_op | source)
XLA Modules:
  0.0 58.1 jit_solution(5143704291515077963)
XLA Ops:
  0.0 0.0 copy-start
  0.0 0.9 %constant_dynamic-slice_fusion.2 = (s32[1,512]{1,0:T(1,128)S(1)}, s32[1,512]{1,0:T(1,128)S(1)}) fusion(s32[8,512]{1,0:T(8,128)} %param.7, s32[]{:T(128)S(6)} %select_n.68, s32[8,512]{1,0:T(8,128)} %param.6), kind=kLoop, calls=%fused_computation.63 | loop fusion | bytes 8196 | tf_op jit(solution)/shard_map/jit(dynamic_index_in_dim)/dynamic_slice | solution.py:218
  0.9 0.2 select_reduce_fusion
  1.1 0.1 reshape.202
  1.3 0.2 reduce_window_sum.11
  1.5 0.1 copy.19
  1.5 0.1 copy.21
  1.6 0.1 compare_and_fusion
  1.7 0.1 copy.18
  1.8 0.1 add_minimum_fusion
  1.8 0.1 min.52
  2.0 0.1 convert_reduce_fusion
  2.0 0.1 select_reduce_fusion.1
  2.1 0.1 copy.20
  2.2 0.1 copy.22
  2.4 0.4 convert_convert_fusion
  2.8 0.0 copy-done
  2.8 2.2 %fusion.11.proj_ref = bf16[12,512,128]{2,1,0:T(8,128)(2,1)} fusion(bf16[12,512,128]{2,1,0:T(8,128)(2,1)S(1)} %copy-done, s32[512]{0:T(512)S(1)} %bitcast.51), kind=kOutput, calls=%fused_computation.13 | convolution fusion | flops 806354944 | bytes 3147776 | tf_op jit(solution)/shard_map/rk,vkd->vrd/dot_general | solution.py:223
  5.0 6.0 %shard_map.46 = bf16[3,512,1024]{2,1,0:T(8,128)(2,1)} custom-call(bf16[12,512,128]{2,1,0:T(8,128)(2,1)} %fusion.11.proj_ref, bf16[6,256,1024]{2,1,0:T(8,128)(2,1)} %tiles_ref.1), custom_call_target="tpu_custom_call" | custom-call | tf_op jit(solution)/shard_map/pallas_call | solution.py:199
  11.0 0.0 copy-start.1
  11.0 4.1 %bitcast_reduce_fusion = f32[8,8,128,21]{2,3,1,0:T(8,128)} fusion(bf16[3,8,8,8,8,128]{5,3,4,2,1,0:T(8,128)(2,1)} %bitcast.45, bf16[8,8,43,8,8]{2,3,4,1,0:T(8,128)(2,1)S(1)} %convert_convert_fusion), kind=kOutput, calls=%fused_computation.7 | convolution fusion | flops 66404352 | bytes 4186112 | tf_op jit(solution)/shard_map/yzbmc,pyzmcl->pyzbl/dot_general | solution.py:245
  15.1 0.0 copy-done.1
  15.1 1.6 %bitcast_reduce_fusion.1 = f32[8,8,128,22]{2,3,1,0:T(8,128)} fusion(bf16[3,8,8,8,8,128]{5,3,4,2,1,0:T(8,128)(2,1)S(1)} %bitcast.46, bf16[8,8,43,8,8]{2,3,4,1,0:T(8,128)(2,1)S(1)} %convert_convert_fusion), kind=kOutput, calls=%fused_computation.8 | convolution fusion | flops 69566464 | bytes 4218880 | tf_op jit(solution)/shard_map/yzbmc,pyzmcl->pyzbl/dot_general | solution.py:243
  16.7 37.4 %shard_map.47 = (f32[22,128]{1,0:T(8,128)}, f32[21,128]{1,0:T(8,128)}) custom-call(f32[8,8,22,128]{3,2,1,0:T(8,128)} %bitcast.48, f32[8,8,21,128]{3,2,1,0:T(8,128)} %bitcast.47), custom_call_target="tpu_custom_call" | custom-call | tf_op jit(solution)/shard_map/pallas_call | solution.py:169
  54.2 0.7 %pad_maximum_fusion = f32[43,128]{1,0:T(8,128)S(1)} fusion(f32[21,128]{1,0:T(8,128)} %get-tuple-element.8, f32[22,128]{1,0:T(8,128)} %get-tuple-element.7), kind=kLoop, calls=%fused_computation.47 | loop fusion | flops 5504 | bytes 44032 | tf_op jit(solution)/shard_map/concatenate | solution.py:248
  54.9 0.6 %gather_fusion = f32[64,128]{1,0:T(8,128)S(1)} fusion(f32[43,128]{1,0:T(8,128)S(1)} %pad_maximum_fusion, s32[1024]{0:T(1024)S(1)} %pad_clamp_fusion), kind=kCustom, calls=%fused_computation | custom fusion | bytes 65792 | tf_op jit(solution)/shard_map/jit(_take)/gather | solution.py:254
  55.5 2.6 %fusion.14 = f32[1,8,1024]{2,1,0:T(8,128)} fusion(f32[8,1024]{1,0:T(8,128)S(1)} %gather.7, f32[1024]{0:T(1024)S(1)} %iota_add_fusion, f32[8]{0:T(128)S(1)} %fusion.35, pred[8,8]{0,1:T(8,128)(4,1)S(1)} %copy.18), kind=kOutput, calls=%fused_computation.16 | convolution fusion | flops 53592064 | bytes 69728 | tf_op jit(solution)/shard_map/dot_general | solution.py:33
  (12 shorter events, 0.2 us)
Async XLA Ops:
  0.0 2.8 %copy-start = (bf16[12,512,128]{2,1,0:T(8,128)(2,1)S(1)}, bf16[12,512,128]{2,1,0:T(8,128)(2,1)}, u32[]{:S(2)}) copy-start(bf16[12,512,128]{2,1,0:T(8,128)(2,1)} %param.4) | copy-start | bytes 4718596
  11.0 4.1 %copy-start.1 = (bf16[3,512,1024]{2,1,0:T(8,128)(2,1)S(1)}, bf16[3,512,1024]{2,1,0:T(8,128)(2,1)}, u32[]{:S(2)}) copy-start(bf16[3,512,1024]{2,1,0:T(8,128)(2,1)} %shard_map.46) | copy-start | bytes 9437188

commit v11 on v10

--- a/solution.py
+++ b/solution.py
@@ -179,26 +179,26 @@
 
 
 def sums_kernel(proj_ref, tiles_ref, out_ref):
-    blocks, pair, samples = tiles_ref.shape
-    footprint = proj_ref.shape[2]
-    per = pair // footprint
-    total = None
-    for b in range(blocks):
-        lhs = jnp.concatenate([proj_ref[b * per + h] for h in range(per)], axis=1)
-        term = jnp.dot(lhs, tiles_ref[b], preferred_element_type=jnp.float32)
-        total = term if total is None else total + term
-    hi = total.astype(jnp.bfloat16)
-    rest = total - hi.astype(jnp.float32)
-    mid = rest.astype(jnp.bfloat16)
-    out_ref[0] = hi
-    out_ref[1] = mid
-    out_ref[2] = (rest - mid.astype(jnp.float32)).astype(jnp.bfloat16)
+    views = proj_ref.shape[0]
+    samples = tiles_ref.shape[1]
+    lhs = jnp.concatenate([proj_ref[v] for v in range(views)], axis=1)
+    width = min(samples, 256)
+    for cb in range(samples // width):
+        cols = pl.ds(cb * width, width)
+        total = jnp.dot(lhs, tiles_ref[:, cols], preferred_element_type=jnp.float32)
+        hi = total.astype(jnp.bfloat16)
+        rest = total - hi.astype(jnp.float32)
+        mid = rest.astype(jnp.bfloat16)
+        out_ref[0, :, cols] = hi
+        out_ref[1, :, cols] = mid
+        out_ref[2, :, cols] = (rest - mid.astype(jnp.float32)).astype(jnp.bfloat16)
 
 
 def owner_sums(proj, tiles):
+    tiles = tiles.reshape(-1, tiles.shape[2])
     return pl.pallas_call(
         sums_kernel,
-        out_shape=jax.ShapeDtypeStruct((3, proj.shape[1], tiles.shape[2]), jnp.bfloat16),
+        out_shape=jax.ShapeDtypeStruct((3, proj.shape[1], tiles.shape[1]), jnp.bfloat16),
         in_specs=[pl.BlockSpec(memory_space=pltpu.VMEM)] * 2,
         out_specs=pl.BlockSpec(memory_space=pltpu.VMEM),
     )(proj, tiles)

time: 58.4 us -> 58.4 us (level)
  no operation moved by 1% of the time
where the time goes in v11:
time: 58.4 us; the launch traced here: 58.1 us
  Pallas kernels  43.4 us (74%)
  matrix products  10.5 us (18%)
  local copies, waits for them, and re-layouts  2.03 us (3%)
  other arithmetic  2 us (3%)
    pallas_call x1, Pallas kernels, reduce_scatter(): pl.pallas_call(functools.partial(rs_kernel, ny, nz), out_shape=(jax.Shape...  37.4 us
    pallas_call x1, Pallas kernels, owner_sums(): pl.pallas_call(sums_kernel, out_shape=jax.ShapeDtypeStruct((3, proj.shape...  6.02 us
    dot_general x1, matrix products, per_device(): jnp.einsum('yzbmc,pyzmcl->pyzbl', choose[:, :, half:], parts, preferred_e...  4.11 us
    dot_general x1, matrix products, invert_block(): jnp.dot(scaled, table.T, precision=lax.Precision.HIGH, preferred_element_...  2.59 us
    dot_general x1, matrix products, per_device(): jnp.einsum('rk,vkd->vrd', perm, proj, preferred_element_type=jnp.float32)  2.17 us
    dot_general x1, matrix products, per_device(): jnp.einsum('yzbmc,pyzmcl->pyzbl', choose[:, :, :half], parts, preferred_e...  1.64 us

profile of v11, /device:TPU:6, one launch (start us, length us, event | category | flops | bytes accessed | tf_op | source)
XLA Modules:
  0.0 58.1 jit_solution(7177732459598699581)
XLA Ops:
  0.0 0.0 copy-start
  0.0 0.9 %constant_dynamic-slice_fusion.2 = (s32[1,512]{1,0:T(1,128)S(1)}, s32[1,512]{1,0:T(1,128)S(1)}) fusion(s32[8,512]{1,0:T(8,128)} %param.7, s32[]{:T(128)S(6)} %select_n.68, s32[8,512]{1,0:T(8,128)} %param.6), kind=kLoop, calls=%fused_computation.63 | loop fusion | bytes 8196 | tf_op jit(solution)/shard_map/jit(dynamic_index_in_dim)/dynamic_slice | solution.py:218
  0.9 0.2 select_reduce_fusion
  1.1 0.1 reshape.205
  1.3 0.2 reduce_window_sum.11
  1.5 0.1 copy.19
  1.5 0.1 copy.21
  1.6 0.1 compare_and_fusion
  1.7 0.1 copy.18
  1.8 0.1 add_minimum_fusion
  1.8 0.1 min.52
  2.0 0.1 convert_reduce_fusion
  2.0 0.1 select_reduce_fusion.1
  2.1 0.1 copy.20
  2.2 0.1 copy.22
  2.4 0.4 convert_convert_fusion
  2.8 0.0 copy-done
  2.8 2.2 %fusion.11.proj_ref = bf16[12,512,128]{2,1,0:T(8,128)(2,1)} fusion(bf16[12,512,128]{2,1,0:T(8,128)(2,1)S(1)} %copy-done, s32[512]{0:T(512)S(1)} %bitcast.53), kind=kOutput, calls=%fused_computation.13 | convolution fusion | flops 806354944 | bytes 3147776 | tf_op jit(solution)/shard_map/rk,vkd->vrd/dot_general | solution.py:223
  5.0 6.0 %shard_map.46 = bf16[3,512,1024]{2,1,0:T(8,128)(2,1)} custom-call(bf16[12,512,128]{2,1,0:T(8,128)(2,1)} %fusion.11.proj_ref, bf16[1536,1024]{1,0:T(8,128)(2,1)} %bitcast.46), custom_call_target="tpu_custom_call" | custom-call | tf_op jit(solution)/shard_map/pallas_call | solution.py:199
  11.0 0.0 copy-start.1
  11.0 4.1 %bitcast_reduce_fusion = f32[8,8,128,21]{2,3,1,0:T(8,128)} fusion(bf16[3,8,8,8,8,128]{5,3,4,2,1,0:T(8,128)(2,1)} %bitcast.47, bf16[8,8,43,8,8]{2,3,4,1,0:T(8,128)(2,1)S(1)} %convert_convert_fusion), kind=kOutput, calls=%fused_computation.7 | convolution fusion | flops 66404352 | bytes 4186112 | tf_op jit(solution)/shard_map/yzbmc,pyzmcl->pyzbl/dot_general | solution.py:245
  15.1 0.0 copy-done.1
  15.1 1.6 %bitcast_reduce_fusion.1 = f32[8,8,128,22]{2,3,1,0:T(8,128)} fusion(bf16[3,8,8,8,8,128]{5,3,4,2,1,0:T(8,128)(2,1)S(1)} %bitcast.48, bf16[8,8,43,8,8]{2,3,4,1,0:T(8,128)(2,1)S(1)} %convert_convert_fusion), kind=kOutput, calls=%fused_computation.8 | convolution fusion | flops 69566464 | bytes 4218880 | tf_op jit(solution)/shard_map/yzbmc,pyzmcl->pyzbl/dot_general | solution.py:243
  16.8 37.4 %shard_map.47 = (f32[22,128]{1,0:T(8,128)}, f32[21,128]{1,0:T(8,128)}) custom-call(f32[8,8,22,128]{3,2,1,0:T(8,128)} %bitcast.50, f32[8,8,21,128]{3,2,1,0:T(8,128)} %bitcast.49), custom_call_target="tpu_custom_call" | custom-call | tf_op jit(solution)/shard_map/pallas_call | solution.py:169
  54.2 0.7 %pad_maximum_fusion = f32[43,128]{1,0:T(8,128)S(1)} fusion(f32[21,128]{1,0:T(8,128)} %get-tuple-element.8, f32[22,128]{1,0:T(8,128)} %get-tuple-element.7), kind=kLoop, calls=%fused_computation.47 | loop fusion | flops 5504 | bytes 44032 | tf_op jit(solution)/shard_map/concatenate | solution.py:248
  54.9 0.6 %gather_fusion = f32[64,128]{1,0:T(8,128)S(1)} fusion(f32[43,128]{1,0:T(8,128)S(1)} %pad_maximum_fusion, s32[1024]{0:T(1024)S(1)} %pad_clamp_fusion), kind=kCustom, calls=%fused_computation | custom fusion | bytes 65792 | tf_op jit(solution)/shard_map/jit(_take)/gather | solution.py:254
  55.5 2.6 %fusion.14 = f32[1,8,1024]{2,1,0:T(8,128)} fusion(f32[8,1024]{1,0:T(8,128)S(1)} %gather.7, f32[1024]{0:T(1024)S(1)} %iota_add_fusion, f32[8]{0:T(128)S(1)} %fusion.35, pred[8,8]{0,1:T(8,128)(4,1)S(1)} %copy.18), kind=kOutput, calls=%fused_computation.16 | convolution fusion | flops 53592064 | bytes 69728 | tf_op jit(solution)/shard_map/dot_general | solution.py:33
  (12 shorter events, 0.2 us)
Async XLA Ops:
  0.0 2.8 %copy-start = (bf16[12,512,128]{2,1,0:T(8,128)(2,1)S(1)}, bf16[12,512,128]{2,1,0:T(8,128)(2,1)}, u32[]{:S(2)}) copy-start(bf16[12,512,128]{2,1,0:T(8,128)(2,1)} %param.4) | copy-start | bytes 4718596
  11.0 4.1 %copy-start.1 = (bf16[3,512,1024]{2,1,0:T(8,128)(2,1)S(1)}, bf16[3,512,1024]{2,1,0:T(8,128)(2,1)}, u32[]{:S(2)}) copy-start(bf16[3,512,1024]{2,1,0:T(8,128)(2,1)} %shard_map.46) | copy-start | bytes 9437188

commit v12 on v11

--- a/solution.py
+++ b/solution.py
@@ -97,7 +97,7 @@
         copy.wait()
 
 
-def rs_kernel(ny, nz, xa, xb, oa, ob, s1a, s1b, *bufs):
+def rs_kernel(ny, nz, xa, xb, out, s1a, s1b, *bufs):
     ssem, rsem = bufs[-2:]
     bufs = bufs[:-2]
     view = lax.axis_index("view")
@@ -149,8 +149,9 @@
         dict(n=nz, me=z, dev=lambda d: dev(y, d), chunk=s1b, recv=recv_b,
              ssem=ssem, rsem=rsem, base=2 * (nz + ny - 2) + ny - 1),
     ])
-    oa[...] = s1a[y] + jnp.sum(recv_a[...], axis=0)
-    ob[...] = s1b[z] + jnp.sum(recv_b[...], axis=0)
+    ra = xa.shape[2]
+    out[pl.ds(0, ra), :] = s1a[y] + jnp.sum(recv_a[...], axis=0)
+    out[pl.ds(ra, xb.shape[2]), :] = s1b[z] + jnp.sum(recv_b[...], axis=0)
 
 
 def reduce_scatter(xa, xb, ny, nz):
@@ -168,9 +169,9 @@
     )
     return pl.pallas_call(
         functools.partial(rs_kernel, ny, nz),
-        out_shape=(jax.ShapeDtypeStruct((ra, LANES), f32), jax.ShapeDtypeStruct((rb, LANES), f32)),
+        out_shape=jax.ShapeDtypeStruct((ra + rb, LANES), f32),
         in_specs=[pl.BlockSpec(memory_space=pltpu.VMEM)] * 2,
-        out_specs=(pl.BlockSpec(memory_space=pltpu.VMEM),) * 2,
+        out_specs=pl.BlockSpec(memory_space=pltpu.VMEM),
         scratch_shapes=[pltpu.VMEM((ny, ra, LANES), f32), pltpu.VMEM((nz, rb, LANES), f32)]
         + bufs
         + [pltpu.SemaphoreType.DMA((3 * (nz + ny - 2),)), pltpu.SemaphoreType.DMA((3 * (nz + ny - 2),))],
@@ -245,7 +246,7 @@
     xb = jnp.einsum("yzbmc,pyzmcl->pyzbl", choose[:, :, half:], parts,
                     preferred_element_type=jnp.float32).sum(axis=0)
 
-    mine = jnp.concatenate(reduce_scatter(xa, xb, ny, nz), axis=0)
+    mine = reduce_scatter(xa, xb, ny, nz)
 
     my_starts = lax.dynamic_index_in_dim(starts, view_place, 0, keepdims=False)
     my_len = lax.dynamic_index_in_dim(order_len, view_place, 0, keepdims=False)

time: 58.4 us -> 58.3 us (level)
  local copies, waits for them, and re-layouts: 2.03 us -> 2.77 us
  other arithmetic: 2 us -> 1.27 us
    gather x2, local copies, waits for them, and re-layouts: 0.61 us -> 1.35 us  [per_device(): rows = jnp.take(mine, back.reshape(-1), axis=0).reshape(owned, samples)]
    concatenate x1 -> x0, other arithmetic: 0.73 us -> none  [per_device(): mine = jnp.concatenate(reduce_scatter(xa, xb, ny, nz), axis=0)]
where the time goes in v12:
time: 58.3 us; the launch traced here: 58.1 us
  Pallas kernels  43.4 us (74%)
  matrix products  10.5 us (18%)
  local copies, waits for them, and re-layouts  2.77 us (5%)
  other arithmetic  1.27 us (2%)
    pallas_call x1, Pallas kernels, reduce_scatter(): pl.pallas_call(functools.partial(rs_kernel, ny, nz), out_shape=jax.ShapeD...  37.4 us
    pallas_call x1, Pallas kernels, owner_sums(): pl.pallas_call(sums_kernel, out_shape=jax.ShapeDtypeStruct((3, proj.shape...  6.02 us
    dot_general x1, matrix products, per_device(): jnp.einsum('yzbmc,pyzmcl->pyzbl', choose[:, :, half:], parts, preferred_e...  4.11 us
    dot_general x1, matrix products, invert_block(): jnp.dot(scaled, table.T, precision=lax.Precision.HIGH, preferred_element_...  2.59 us
    dot_general x1, matrix products, per_device(): jnp.einsum('rk,vkd->vrd', perm, proj, preferred_element_type=jnp.float32)  2.17 us
    dot_general x1, matrix products, per_device(): jnp.einsum('yzbmc,pyzmcl->pyzbl', choose[:, :, :half], parts, preferred_e...  1.64 us
    gather x2, local copies, waits for them, and re-layouts, per_device(): rows = jnp.take(mine, back.reshape(-1), axis=0).reshape(owned, samples)  1.35 us

profile of v12, /device:TPU:6, one launch (start us, length us, event | category | flops | bytes accessed | tf_op | source)
XLA Modules:
  0.0 58.1 jit_solution(12078290836576713712)
XLA Ops:
  0.0 0.0 copy-start
  0.0 0.9 %constant_dynamic-slice_fusion.2 = (s32[1,512]{1,0:T(1,128)S(1)}, s32[1,512]{1,0:T(1,128)S(1)}) fusion(s32[8,512]{1,0:T(8,128)} %param.7, s32[]{:T(128)S(6)} %select_n.68, s32[8,512]{1,0:T(8,128)} %param.6), kind=kLoop, calls=%fused_computation.62 | loop fusion | bytes 8196 | tf_op jit(solution)/shard_map/jit(dynamic_index_in_dim)/dynamic_slice | solution.py:219
  0.9 0.2 select_reduce_fusion
  1.1 0.1 reshape.205
  1.3 0.2 reduce_window_sum.11
  1.5 0.1 copy.19
  1.5 0.1 copy.21
  1.6 0.1 compare_and_fusion
  1.7 0.1 copy.18
  1.8 0.1 add_minimum_fusion
  1.8 0.1 min.52
  2.0 0.1 convert_reduce_fusion
  2.0 0.1 select_reduce_fusion.1
  2.1 0.1 copy.20
  2.2 0.1 copy.22
  2.4 0.4 convert_convert_fusion
  2.8 0.0 copy-done
  2.8 2.2 %fusion.11.proj_ref = bf16[12,512,128]{2,1,0:T(8,128)(2,1)} fusion(bf16[12,512,128]{2,1,0:T(8,128)(2,1)S(1)} %copy-done, s32[512]{0:T(512)S(1)} %bitcast.53), kind=kOutput, calls=%fused_computation.13 | convolution fusion | flops 806354944 | bytes 3147776 | tf_op jit(solution)/shard_map/rk,vkd->vrd/dot_general | solution.py:224
  5.0 6.0 %shard_map.46 = bf16[3,512,1024]{2,1,0:T(8,128)(2,1)} custom-call(bf16[12,512,128]{2,1,0:T(8,128)(2,1)} %fusion.11.proj_ref, bf16[1536,1024]{1,0:T(8,128)(2,1)} %bitcast.46), custom_call_target="tpu_custom_call" | custom-call | tf_op jit(solution)/shard_map/pallas_call | solution.py:200
  11.0 0.0 copy-start.1
  11.0 4.1 %bitcast_reduce_fusion = f32[8,8,128,21]{2,3,1,0:T(8,128)} fusion(bf16[3,8,8,8,8,128]{5,3,4,2,1,0:T(8,128)(2,1)} %bitcast.47, bf16[8,8,43,8,8]{2,3,4,1,0:T(8,128)(2,1)S(1)} %convert_convert_fusion), kind=kOutput, calls=%fused_computation.7 | convolution fusion | flops 66404352 | bytes 4186112 | tf_op jit(solution)/shard_map/yzbmc,pyzmcl->pyzbl/dot_general | solution.py:246
  15.1 0.0 copy-done.1
  15.1 1.6 %bitcast_reduce_fusion.1 = f32[8,8,128,22]{2,3,1,0:T(8,128)} fusion(bf16[3,8,8,8,8,128]{5,3,4,2,1,0:T(8,128)(2,1)S(1)} %bitcast.48, bf16[8,8,43,8,8]{2,3,4,1,0:T(8,128)(2,1)S(1)} %convert_convert_fusion), kind=kOutput, calls=%fused_computation.8 | convolution fusion | flops 69566464 | bytes 4218880 | tf_op jit(solution)/shard_map/yzbmc,pyzmcl->pyzbl/dot_general | solution.py:244
  16.8 37.4 %shard_map.47 = f32[43,128]{1,0:T(8,128)} custom-call(f32[8,8,22,128]{3,2,1,0:T(8,128)} %bitcast.50, f32[8,8,21,128]{3,2,1,0:T(8,128)} %bitcast.49), custom_call_target="tpu_custom_call" | custom-call | tf_op jit(solution)/shard_map/pallas_call | solution.py:170
  54.2 1.3 %gather_fusion = f32[64,128]{1,0:T(8,128)S(1)} fusion(f32[43,128]{1,0:T(8,128)} %shard_map.47, s32[1024]{0:T(1024)S(1)} %pad_clamp_fusion), kind=kCustom, calls=%fused_computation | custom fusion | bytes 65792 | tf_op jit(solution)/shard_map/jit(_take)/gather | solution.py:255
  55.5 2.6 %fusion.14 = f32[1,8,1024]{2,1,0:T(8,128)} fusion(f32[8,1024]{1,0:T(8,128)S(1)} %gather.7, f32[1024]{0:T(1024)S(1)} %iota_add_fusion, f32[8]{0:T(128)S(1)} %fusion.35, pred[8,8]{0,1:T(8,128)(4,1)S(1)} %copy.18), kind=kOutput, calls=%fused_computation.16 | convolution fusion | flops 53592064 | bytes 69728 | tf_op jit(solution)/shard_map/dot_general | solution.py:33
  (12 shorter events, 0.2 us)
Async XLA Ops:
  0.0 2.8 %copy-start = (bf16[12,512,128]{2,1,0:T(8,128)(2,1)S(1)}, bf16[12,512,128]{2,1,0:T(8,128)(2,1)}, u32[]{:S(2)}) copy-start(bf16[12,512,128]{2,1,0:T(8,128)(2,1)} %param.4) | copy-start | bytes 4718596
  11.0 4.1 %copy-start.1 = (bf16[3,512,1024]{2,1,0:T(8,128)(2,1)S(1)}, bf16[3,512,1024]{2,1,0:T(8,128)(2,1)}, u32[]{:S(2)}) copy-start(bf16[3,512,1024]{2,1,0:T(8,128)(2,1)} %shard_map.46) | copy-start | bytes 9437188

commit v13 on v12

--- a/solution.py
+++ b/solution.py
@@ -97,7 +97,7 @@
         copy.wait()
 
 
-def rs_kernel(ny, nz, xa, xb, out, s1a, s1b, *bufs):
+def rs_kernel(ny, nz, ra, x, out, s1a, s1b, *bufs):
     ssem, rsem = bufs[-2:]
     bufs = bufs[:-2]
     view = lax.axis_index("view")
@@ -120,12 +120,15 @@
         pl.semaphore_signal(barrier, inc=1, device_id=dev(y, lax.rem(z + k, nz)), device_id_type=MESH)
     pl.semaphore_wait(barrier, ny + nz - 2)
 
+    rows_a = pl.ds(0, ra)
+    rows_b = pl.ds(ra, x.shape[2] - ra)
+
     def ring(n, me, right, left, x, part, at, base, swap=False):
         rr, rl, sr, sl = bufs[4 * at: 4 * at + 4]
         if swap:
-            src, val = (lambda d: x.at[part, d]), (lambda d: x[part, d])
+            src, val = (lambda d: x.at[part, d, rows_a]), (lambda d: x[part, d, rows_a])
         else:
-            src, val = (lambda d: x.at[d, part]), (lambda d: x[d, part])
+            src, val = (lambda d: x.at[d, part, rows_b]), (lambda d: x[d, part, rows_b])
         return dict(n=n, me=me, right=right, left=left, rr=rr, rl=rl, sr=sr, sl=sl,
                     src=src, val=val, ssem=ssem, rsem=rsem, base=base)
 
@@ -133,15 +136,15 @@
     lo_a, hi_a = pl.ds(0, ha), pl.ds(ha, ny - ha)
     lo_b, hi_b = pl.ds(0, hb), pl.ds(hb, nz - hb)
     fins = run_rings([
-        ring(nz, z, z_right, z_left, xa, lo_a, 0, 0, swap=True),
-        ring(nz, z, z_right, z_left, xa, hi_a, 1, nz - 1, swap=True),
-        ring(ny, y, y_right, y_left, xb, lo_b, 2, 2 * (nz - 1)),
-        ring(ny, y, y_right, y_left, xb, hi_b, 3, 2 * (nz - 1) + ny - 1),
+        ring(nz, z, z_right, z_left, x, lo_a, 0, 0, swap=True),
+        ring(nz, z, z_right, z_left, x, hi_a, 1, nz - 1, swap=True),
+        ring(ny, y, y_right, y_left, x, lo_b, 2, 2 * (nz - 1)),
+        ring(ny, y, y_right, y_left, x, hi_b, 3, 2 * (nz - 1) + ny - 1),
     ])
-    s1a[lo_a] = xa[lo_a, z] + fins[0][0][...] + fins[0][1][...]
-    s1a[hi_a] = xa[hi_a, z] + fins[1][0][...] + fins[1][1][...]
-    s1b[lo_b] = xb[y, lo_b] + fins[2][0][...] + fins[2][1][...]
-    s1b[hi_b] = xb[y, hi_b] + fins[3][0][...] + fins[3][1][...]
+    s1a[lo_a] = x[lo_a, z, rows_a] + fins[0][0][...] + fins[0][1][...]
+    s1a[hi_a] = x[hi_a, z, rows_a] + fins[1][0][...] + fins[1][1][...]
+    s1b[lo_b] = x[y, lo_b, rows_b] + fins[2][0][...] + fins[2][1][...]
+    s1b[hi_b] = x[y, hi_b, rows_b] + fins[3][0][...] + fins[3][1][...]
     recv_a, recv_b = bufs[16], bufs[17]
     run_direct([
         dict(n=ny, me=y, dev=lambda d: dev(d, z), chunk=s1a, recv=recv_a,
@@ -149,13 +152,12 @@
         dict(n=nz, me=z, dev=lambda d: dev(y, d), chunk=s1b, recv=recv_b,
              ssem=ssem, rsem=rsem, base=2 * (nz + ny - 2) + ny - 1),
     ])
-    ra = xa.shape[2]
-    out[pl.ds(0, ra), :] = s1a[y] + jnp.sum(recv_a[...], axis=0)
-    out[pl.ds(ra, xb.shape[2]), :] = s1b[z] + jnp.sum(recv_b[...], axis=0)
-
-
-def reduce_scatter(xa, xb, ny, nz):
-    ra, rb = xa.shape[2], xb.shape[2]
+    out[rows_a, :] = s1a[y] + jnp.sum(recv_a[...], axis=0)
+    out[rows_b, :] = s1b[z] + jnp.sum(recv_b[...], axis=0)
+
+
+def reduce_scatter(x, ra, ny, nz):
+    rb = x.shape[2] - ra
     f32 = jnp.float32
 
     def slots(n, shape):
@@ -168,15 +170,15 @@
         + [pltpu.VMEM((ny - 1, ra, LANES), f32), pltpu.VMEM((nz - 1, rb, LANES), f32)]
     )
     return pl.pallas_call(
-        functools.partial(rs_kernel, ny, nz),
+        functools.partial(rs_kernel, ny, nz, ra),
         out_shape=jax.ShapeDtypeStruct((ra + rb, LANES), f32),
-        in_specs=[pl.BlockSpec(memory_space=pltpu.VMEM)] * 2,
+        in_specs=[pl.BlockSpec(memory_space=pltpu.VMEM)],
         out_specs=pl.BlockSpec(memory_space=pltpu.VMEM),
         scratch_shapes=[pltpu.VMEM((ny, ra, LANES), f32), pltpu.VMEM((nz, rb, LANES), f32)]
         + bufs
         + [pltpu.SemaphoreType.DMA((3 * (nz + ny - 2),)), pltpu.SemaphoreType.DMA((3 * (nz + ny - 2),))],
         compiler_params=pltpu.CompilerParams(collective_id=0, has_side_effects=True),
-    )(xa, xb)
+    )(x)
 
 
 def sums_kernel(proj_ref, tiles_ref, out_ref):
@@ -241,12 +243,10 @@
         & (within[..., None, None] == jnp.arange(chunks_per_row, dtype=jnp.int32)[None, :])
     ).astype(jnp.float32)
     choose = choose.astype(jnp.bfloat16)
-    xa = jnp.einsum("yzbmc,pyzmcl->pyzbl", choose[:, :, :half], parts,
-                    preferred_element_type=jnp.float32).sum(axis=0)
-    xb = jnp.einsum("yzbmc,pyzmcl->pyzbl", choose[:, :, half:], parts,
-                    preferred_element_type=jnp.float32).sum(axis=0)
-
-    mine = reduce_scatter(xa, xb, ny, nz)
+    x = jnp.einsum("yzbmc,pyzmcl->pyzbl", choose, parts,
+                   preferred_element_type=jnp.float32).sum(axis=0)
+
+    mine = reduce_scatter(x, half, ny, nz)
 
     my_starts = lax.dynamic_index_in_dim(starts, view_place, 0, keepdims=False)
     my_len = lax.dynamic_index_in_dim(order_len, view_place, 0, keepdims=False)

time: 58.3 us -> 56.3 us (0.966)
  matrix products: 10.5 us -> 8.8 us
    dot_general x2 -> x1, matrix products: 5.75 us -> 4.04 us  [per_device(): jnp.einsum('yzbmc,pyzmcl->pyzbl', choose, parts, preferred_element_type=j...]
where the time goes in v13:
time: 56.3 us; the launch traced here: 56.1 us
  Pallas kernels  43.5 us (77%)
  matrix products  8.8 us (16%)
  local copies, waits for them, and re-layouts  2.77 us (5%)
  other arithmetic  0.88 us (2%)
    pallas_call x1, Pallas kernels, reduce_scatter(): pl.pallas_call(functools.partial(rs_kernel, ny, nz, ra), out_shape=jax.Sh...  37.5 us
    pallas_call x1, Pallas kernels, owner_sums(): pl.pallas_call(sums_kernel, out_shape=jax.ShapeDtypeStruct((3, proj.shape...  6.02 us
    dot_general x1, matrix products, per_device(): jnp.einsum('yzbmc,pyzmcl->pyzbl', choose, parts, preferred_element_type=j...  4.04 us
    dot_general x1, matrix products, invert_block(): jnp.dot(scaled, table.T, precision=lax.Precision.HIGH, preferred_element_...  2.59 us
    dot_general x1, matrix products, per_device(): jnp.einsum('rk,vkd->vrd', perm, proj, preferred_element_type=jnp.float32)  2.17 us
    gather x2, local copies, waits for them, and re-layouts, per_device(): rows = jnp.take(mine, back.reshape(-1), axis=0).reshape(owned, samples)  1.35 us

profile of v13, /device:TPU:6, one launch (start us, length us, event | category | flops | bytes accessed | tf_op | source)
XLA Modules:
  0.0 56.1 jit_solution(5373637310979056244)
XLA Ops:
  0.0 0.0 copy-start
  0.0 0.9 %constant_dynamic-slice_fusion.2 = (s32[1,512]{1,0:T(1,128)S(1)}, s32[1,512]{1,0:T(1,128)S(1)}) fusion(s32[8,512]{1,0:T(8,128)} %param.7, s32[]{:T(128)S(6)} %select_n.68, s32[8,512]{1,0:T(8,128)} %param.6), kind=kLoop, calls=%fused_computation.60 | loop fusion | bytes 8196 | tf_op jit(solution)/shard_map/jit(dynamic_index_in_dim)/dynamic_slice | solution.py:221
  0.9 0.2 select_reduce_fusion
  1.1 0.1 reshape.205
  1.3 0.2 reduce_window_sum.11
  1.5 0.1 copy.16
  1.5 0.1 copy.18
  1.6 0.1 compare_and_fusion
  1.7 0.1 copy.15
  1.8 0.1 add_minimum_fusion
  1.8 0.1 min.52
  2.0 0.1 convert_reduce_fusion
  2.0 0.1 select_reduce_fusion.1
  2.1 0.1 copy.17
  2.2 0.1 copy.19
  2.4 0.0 copy-done
  2.4 2.2 %fusion.5.proj_ref = bf16[12,512,128]{2,1,0:T(8,128)(2,1)} fusion(bf16[12,512,128]{2,1,0:T(8,128)(2,1)S(1)} %copy-done, s32[512]{0:T(512)S(1)} %bitcast.42), kind=kOutput, calls=%fused_computation.10 | convolution fusion | flops 806354944 | bytes 3147776 | tf_op jit(solution)/shard_map/rk,vkd->vrd/dot_general | solution.py:226
  4.6 6.0 %shard_map.46 = bf16[3,512,1024]{2,1,0:T(8,128)(2,1)} custom-call(bf16[12,512,128]{2,1,0:T(8,128)(2,1)} %fusion.5.proj_ref, bf16[1536,1024]{1,0:T(8,128)(2,1)} %bitcast.37), custom_call_target="tpu_custom_call" | custom-call | tf_op jit(solution)/shard_map/pallas_call | solution.py:202
  10.6 4.0 %bitcast_reduce_fusion = f32[8,8,128,43]{2,3,1,0:T(8,128)} fusion(bf16[3,8,8,8,8,128]{5,3,4,2,1,0:T(8,128)(2,1)} %bitcast.38, pred[8,8,43,8]{2,3,1,0:T(8,128)(4,1)S(1)} %iota_compare_fusion.2, pred[8,8,43,8]{2,3,1,0:T(8,128)(4,1)S(1)} %iota_compare_fusion.3), kind=kOutput, calls=%fused_computation.1 | convolution fusion | flops 136499200 | bytes 4598784 | tf_op jit(solution)/shard_map/yzbmc,pyzmcl->pyzbl/dot_general | solution.py:246
  14.6 37.5 %shard_map.47 = f32[43,128]{1,0:T(8,128)} custom-call(f32[8,8,43,128]{3,2,1,0:T(8,128)} %bitcast.39), custom_call_target="tpu_custom_call" | custom-call | tf_op jit(solution)/shard_map/pallas_call | solution.py:172
  52.1 1.3 %gather_fusion = f32[64,128]{1,0:T(8,128)S(1)} fusion(f32[43,128]{1,0:T(8,128)} %shard_map.47, s32[1024]{0:T(1024)S(1)} %pad_clamp_fusion), kind=kCustom, calls=%fused_computation | custom fusion | bytes 65792 | tf_op jit(solution)/shard_map/jit(_take)/gather | solution.py:255
  53.5 2.6 %fusion.10 = f32[1,8,1024]{2,1,0:T(8,128)} fusion(f32[8,1024]{1,0:T(8,128)S(1)} %gather.7, f32[1024]{0:T(1024)S(1)} %iota_add_fusion, f32[8]{0:T(128)S(1)} %fusion.35, pred[8,8]{0,1:T(8,128)(4,1)S(1)} %copy.15), kind=kOutput, calls=%fused_computation.13 | convolution fusion | flops 53592064 | bytes 69728 | tf_op jit(solution)/shard_map/dot_general | solution.py:33
  (12 shorter events, 0.2 us)
Async XLA Ops:
  0.0 2.4 %copy-start = (bf16[12,512,128]{2,1,0:T(8,128)(2,1)S(1)}, bf16[12,512,128]{2,1,0:T(8,128)(2,1)}, u32[]{:S(2)}) copy-start(bf16[12,512,128]{2,1,0:T(8,128)(2,1)} %param.4) | copy-start | bytes 4718596

commit v14 on v13

--- a/solution.py
+++ b/solution.py
@@ -243,8 +243,8 @@
         & (within[..., None, None] == jnp.arange(chunks_per_row, dtype=jnp.int32)[None, :])
     ).astype(jnp.float32)
     choose = choose.astype(jnp.bfloat16)
-    x = jnp.einsum("yzbmc,pyzmcl->pyzbl", choose, parts,
-                   preferred_element_type=jnp.float32).sum(axis=0)
+    choose = jnp.broadcast_to(choose[:, :, :, None], choose.shape[:3] + (3,) + choose.shape[3:])
+    x = jnp.einsum("yzbpmc,pyzmcl->yzbl", choose, parts, preferred_element_type=jnp.float32)
 
     mine = reduce_scatter(x, half, ny, nz)
 

time: 56.3 us -> 56.7 us (level)
  no operation moved by 1% of the time
where the time goes in v14:
time: 56.7 us; the launch traced here: 56.4 us
  Pallas kernels  43.5 us (77%)
  matrix products  8.8 us (16%)
  local copies, waits for them, and re-layouts  2.77 us (5%)
  other arithmetic  1.27 us (2%)
    pallas_call x1, Pallas kernels, reduce_scatter(): pl.pallas_call(functools.partial(rs_kernel, ny, nz, ra), out_shape=jax.Sh...  37.4 us
    pallas_call x1, Pallas kernels, owner_sums(): pl.pallas_call(sums_kernel, out_shape=jax.ShapeDtypeStruct((3, proj.shape...  6.02 us
    dot_general x1, matrix products, per_device(): jnp.einsum('yzbpmc,pyzmcl->yzbl', choose, parts, preferred_element_type=j...  4.04 us
    dot_general x1, matrix products, invert_block(): jnp.dot(scaled, table.T, precision=lax.Precision.HIGH, preferred_element_...  2.59 us
    dot_general x1, matrix products, per_device(): jnp.einsum('rk,vkd->vrd', perm, proj, preferred_element_type=jnp.float32)  2.17 us
    gather x2, local copies, waits for them, and re-layouts, per_device(): rows = jnp.take(mine, back.reshape(-1), axis=0).reshape(owned, samples)  1.35 us

profile of v14, /device:TPU:6, one launch (start us, length us, event | category | flops | bytes accessed | tf_op | source)
XLA Modules:
  0.0 56.4 jit_solution(11370683680693664967)
XLA Ops:
  0.0 0.0 copy-start
  0.0 0.9 %constant_dynamic-slice_fusion.2 = (s32[1,512]{1,0:T(1,128)S(1)}, s32[1,512]{1,0:T(1,128)S(1)}) fusion(s32[8,512]{1,0:T(8,128)} %param.7, s32[]{:T(128)S(6)} %select_n.68, s32[8,512]{1,0:T(8,128)} %param.6), kind=kLoop, calls=%fused_computation.58 | loop fusion | bytes 8196 | tf_op jit(solution)/shard_map/jit(dynamic_index_in_dim)/dynamic_slice | solution.py:221
  0.9 0.2 select_reduce_fusion
  1.1 0.1 reshape.208
  1.3 0.2 reduce_window_sum.11
  1.5 0.1 copy.16
  1.5 0.1 copy.18
  1.6 0.1 compare_and_fusion
  1.7 0.1 copy.15
  1.8 0.1 add_minimum_fusion
  1.8 0.1 min.52
  2.0 0.1 convert_reduce_fusion
  2.0 0.1 select_reduce_fusion.1
  2.1 0.1 copy.17
  2.2 0.1 copy.19
  2.4 0.4 convert_convert_fusion
  2.8 0.0 copy-done
  2.8 2.2 %fusion.11.proj_ref = bf16[12,512,128]{2,1,0:T(8,128)(2,1)} fusion(bf16[12,512,128]{2,1,0:T(8,128)(2,1)S(1)} %copy-done, s32[512]{0:T(512)S(1)} %bitcast.36), kind=kOutput, calls=%fused_computation.11 | convolution fusion | flops 806354944 | bytes 3147776 | tf_op jit(solution)/shard_map/rk,vkd->vrd/dot_general | solution.py:226
  5.0 6.0 %shard_map.46 = bf16[3,512,1024]{2,1,0:T(8,128)(2,1)} custom-call(bf16[12,512,128]{2,1,0:T(8,128)(2,1)} %fusion.11.proj_ref, bf16[1536,1024]{1,0:T(8,128)(2,1)} %bitcast.32), custom_call_target="tpu_custom_call" | custom-call | tf_op jit(solution)/shard_map/pallas_call | solution.py:202
  11.0 4.0 %fusion.6.x = f32[8,8,43,128]{3,2,1,0:T(8,128)} fusion(bf16[3,8,8,8,8,128]{5,3,4,2,1,0:T(8,128)(2,1)} %bitcast.33, bf16[8,8,43,8,8]{2,3,4,1,0:T(8,128)(2,1)S(1)} %convert_convert_fusion), kind=kOutput, calls=%fused_computation.10 | convolution fusion | flops 135266304 | bytes 4907008 | tf_op jit(solution)/shard_map/yzbpmc,pyzmcl->yzbl/dot_general | solution.py:247
  15.0 37.4 %shard_map.47 = f32[43,128]{1,0:T(8,128)} custom-call(f32[8,8,43,128]{3,2,1,0:T(8,128)} %fusion.6.x), custom_call_target="tpu_custom_call" | custom-call | tf_op jit(solution)/shard_map/pallas_call | solution.py:172
  52.5 1.3 %gather_fusion = f32[64,128]{1,0:T(8,128)S(1)} fusion(f32[43,128]{1,0:T(8,128)} %shard_map.47, s32[1024]{0:T(1024)S(1)} %pad_clamp_fusion), kind=kCustom, calls=%fused_computation | custom fusion | bytes 65792 | tf_op jit(solution)/shard_map/jit(_take)/gather | solution.py:255
  53.8 2.6 %fusion.14 = f32[1,8,1024]{2,1,0:T(8,128)} fusion(f32[8,1024]{1,0:T(8,128)S(1)} %gather.7, f32[1024]{0:T(1024)S(1)} %iota_add_fusion, f32[8]{0:T(128)S(1)} %fusion.35, pred[8,8]{0,1:T(8,128)(4,1)S(1)} %copy.15), kind=kOutput, calls=%fused_computation.14 | convolution fusion | flops 53592064 | bytes 69728 | tf_op jit(solution)/shard_map/dot_general | solution.py:33
  (12 shorter events, 0.2 us)
Async XLA Ops:
  0.0 2.8 %copy-start = (bf16[12,512,128]{2,1,0:T(8,128)(2,1)S(1)}, bf16[12,512,128]{2,1,0:T(8,128)(2,1)}, u32[]{:S(2)}) copy-start(bf16[12,512,128]{2,1,0:T(8,128)(2,1)} %param.4) | copy-start | bytes 4718596

commit v15 on v13

--- a/solution.py
+++ b/solution.py
@@ -252,10 +252,22 @@
     my_len = lax.dynamic_index_in_dim(order_len, view_place, 0, keepdims=False)
     back = my_starts[:, None] + jnp.arange(chunks_per_row, dtype=jnp.int32)[None, :]
     back = jnp.minimum(back, slots - 1)
-    rows = jnp.take(mine, back.reshape(-1), axis=0).reshape(owned, samples)
-
-    table = kernel_table(samples, 0.0, samples)
-    recon = invert_block(rows, my_len, table, 0.0)
+    rows = jnp.take(mine, back, axis=0, mode="clip")
+
+    length = my_len.astype(jnp.float32)[:, None, None]
+    position = (
+        jnp.arange(chunks_per_row, dtype=jnp.float32)[:, None] * LANES
+        + jnp.arange(LANES, dtype=jnp.float32)[None, :]
+    )[None] + 0.5
+    col_in = position < length
+    col_w = jnp.sqrt(jnp.where(col_in, position * (length - position), 1.0))
+    scaled = jnp.where(col_in, col_w * rows, 0.0)
+    row_pos = jnp.arange(samples, dtype=jnp.float32)[:, None, None]
+    table = 1.0 / (row_pos - (position - 0.5) + 0.5)
+    image = jnp.einsum("mcl,pcl->mp", scaled, table, precision=lax.Precision.HIGH,
+                       preferred_element_type=jnp.float32)
+    row_in, row_w = weigh(my_len.astype(jnp.float32)[:, None], samples, 0.0)
+    recon = jnp.where(row_in, image / (math.pi * row_w), 0.0)
     return recon[None]
 
 

time: 56.3 us -> 56.2 us (level)
    gather x2 -> x1, local copies, waits for them, and re-layouts: 1.35 us -> 1.33 us  [per_device(): rows = jnp.take(mine, back, axis=0, mode='clip')]
where the time goes in v15:
time: 56.2 us; the launch traced here: 55.9 us
  Pallas kernels  43.5 us (77%)
  matrix products  8.8 us (16%)
  local copies, waits for them, and re-layouts  2.67 us (5%)
  other arithmetic  0.89 us (2%)
    pallas_call x1, Pallas kernels, reduce_scatter(): pl.pallas_call(functools.partial(rs_kernel, ny, nz, ra), out_shape=jax.Sh...  37.5 us
    pallas_call x1, Pallas kernels, owner_sums(): pl.pallas_call(sums_kernel, out_shape=jax.ShapeDtypeStruct((3, proj.shape...  6.02 us
    dot_general x1, matrix products, per_device(): jnp.einsum('yzbmc,pyzmcl->pyzbl', choose, parts, preferred_element_type=j...  4.05 us
    dot_general x1, matrix products, per_device(): jnp.einsum('mcl,pcl->mp', scaled, table, precision=lax.Precision.HIGH, pr...  2.58 us
    dot_general x1, matrix products, per_device(): jnp.einsum('rk,vkd->vrd', perm, proj, preferred_element_type=jnp.float32)  2.17 us
    gather x1, local copies, waits for them, and re-layouts, per_device(): rows = jnp.take(mine, back, axis=0, mode='clip')  1.33 us

profile of v15, /device:TPU:6, one launch (start us, length us, event | category | flops | bytes accessed | tf_op | source)
XLA Modules:
  0.0 55.9 jit_solution(15024143410374985002)
XLA Ops:
  0.0 0.0 copy-start
  0.0 0.9 %constant_dynamic-slice_fusion.2 = (s32[1,512]{1,0:T(1,128)S(1)}, s32[1,512]{1,0:T(1,128)S(1)}) fusion(s32[8,512]{1,0:T(8,128)} %param.7, s32[]{:T(128)S(6)} %select_n.49, s32[8,512]{1,0:T(8,128)} %param.6), kind=kLoop, calls=%fused_computation.61 | loop fusion | bytes 8196 | tf_op jit(solution)/shard_map/jit(dynamic_index_in_dim)/dynamic_slice | solution.py:221
  0.9 0.2 select_reduce_fusion
  1.1 0.1 broadcast_add_fusion
  1.2 0.1 reshape.244
  1.4 0.2 reduce_window_sum.11
  1.6 0.1 copy.15
  1.6 0.1 copy.17
  1.7 0.1 add_minimum_fusion
  1.8 0.1 reshape.249
  1.9 0.1 convert_reduce_fusion
  1.9 0.1 select_reduce_fusion.1
  2.0 0.1 copy.16
  2.1 0.1 copy.18
  2.3 0.0 copy-done
  2.3 2.2 %fusion.6.proj_ref = bf16[12,512,128]{2,1,0:T(8,128)(2,1)} fusion(bf16[12,512,128]{2,1,0:T(8,128)(2,1)S(1)} %copy-done, s32[512]{0:T(512)S(1)} %bitcast.47), kind=kOutput, calls=%fused_computation.11 | convolution fusion | flops 806354944 | bytes 3147776 | tf_op jit(solution)/shard_map/rk,vkd->vrd/dot_general | solution.py:226
  4.5 6.0 %shard_map.46 = bf16[3,512,1024]{2,1,0:T(8,128)(2,1)} custom-call(bf16[12,512,128]{2,1,0:T(8,128)(2,1)} %fusion.6.proj_ref, bf16[1536,1024]{1,0:T(8,128)(2,1)} %bitcast.41), custom_call_target="tpu_custom_call" | custom-call | tf_op jit(solution)/shard_map/pallas_call | solution.py:202
  10.5 4.0 %bitcast_reduce_fusion = f32[8,8,128,43]{2,3,1,0:T(8,128)} fusion(bf16[3,8,8,8,8,128]{5,3,4,2,1,0:T(8,128)(2,1)} %bitcast.42, pred[8,8,43,8]{2,3,1,0:T(8,128)(4,1)S(1)} %iota_compare_fusion.2, pred[8,8,43,8]{2,3,1,0:T(8,128)(4,1)S(1)} %iota_compare_fusion.3), kind=kOutput, calls=%fused_computation.1 | convolution fusion | flops 136499200 | bytes 4598784 | tf_op jit(solution)/shard_map/yzbmc,pyzmcl->pyzbl/dot_general | solution.py:246
  14.6 37.5 %shard_map.47 = f32[43,128]{1,0:T(8,128)} custom-call(f32[8,8,43,128]{3,2,1,0:T(8,128)} %bitcast.43), custom_call_target="tpu_custom_call" | custom-call | tf_op jit(solution)/shard_map/pallas_call | solution.py:172
  52.0 1.3 %gather_fusion = f32[64,128]{1,0:T(8,128)S(1)} fusion(f32[43,128]{1,0:T(8,128)} %shard_map.47, s32[1024]{0:T(1024)S(1)} %pad_clamp_fusion), kind=kCustom, calls=%fused_computation | custom fusion | bytes 65792 | tf_op jit(solution)/shard_map/jit(_take)/gather | solution.py:255
  53.4 2.6 %fusion.12 = f32[1,8,1024]{2,1,0:T(8,128)} fusion(f32[8,128]{1,0:T(8,128)S(1)} %get-tuple-element.6, f32[8,8,128]{2,1,0:T(8,128)S(1)} %bitcast.45, f32[8,128]{1,0:T(8,128)S(1)} %get-tuple-element.5, f32[1024]{0:T(1024)S(1)} %iota_add_fusion.1, f32[8]{0:T(128)S(1)} %fusion.36), kind=kOutput, calls=%fused_computation.15 | convolution fusion | flops 53583872 | bytes 77856 | tf_op jit(solution)/shard_map/mcl,pcl->mp/dot_general | solution.py:267
  (11 shorter events, 0.2 us)
Async XLA Ops:
  0.0 2.3 %copy-start = (bf16[12,512,128]{2,1,0:T(8,128)(2,1)S(1)}, bf16[12,512,128]{2,1,0:T(8,128)(2,1)}, u32[]{:S(2)}) copy-start(bf16[12,512,128]{2,1,0:T(8,128)(2,1)} %param.4) | copy-start | bytes 4718596

commit v16 on v15

--- a/solution.py
+++ b/solution.py
@@ -252,7 +252,9 @@
     my_len = lax.dynamic_index_in_dim(order_len, view_place, 0, keepdims=False)
     back = my_starts[:, None] + jnp.arange(chunks_per_row, dtype=jnp.int32)[None, :]
     back = jnp.minimum(back, slots - 1)
-    rows = jnp.take(mine, back, axis=0, mode="clip")
+    hit = (back[:, :, None] == jnp.arange(slots, dtype=jnp.int32)).astype(jnp.float32)
+    rows = jnp.einsum("mcj,jl->mcl", hit, mine, precision=lax.Precision.HIGHEST,
+                      preferred_element_type=jnp.float32)
 
     length = my_len.astype(jnp.float32)[:, None, None]
     position = (

time: 56.2 us -> 56.1 us (level)
  local copies, waits for them, and re-layouts: 2.67 us -> 1.25 us
  matrix products: 8.8 us -> 9.72 us
    gather x1 -> x0, local copies, waits for them, and re-layouts: 1.33 us -> none  [per_device(): rows = jnp.take(mine, back, axis=0, mode='clip')]
    dot_general x0 -> x1, matrix products: none -> 0.94 us  [per_device(): jnp.einsum('mcj,jl->mcl', hit, mine, precision=lax.Precision.HIGHEST, pre...]
where the time goes in v16:
time: 56.1 us; the launch traced here: 55.8 us
  Pallas kernels  43.5 us (78%)
  matrix products  9.72 us (17%)
  local copies, waits for them, and re-layouts  1.25 us (2%)
  other arithmetic  1.2 us (2%)
    pallas_call x1, Pallas kernels, reduce_scatter(): pl.pallas_call(functools.partial(rs_kernel, ny, nz, ra), out_shape=jax.Sh...  37.5 us
    pallas_call x1, Pallas kernels, owner_sums(): pl.pallas_call(sums_kernel, out_shape=jax.ShapeDtypeStruct((3, proj.shape...  6.02 us
    dot_general x1, matrix products, per_device(): jnp.einsum('yzbmc,pyzmcl->pyzbl', choose, parts, preferred_element_type=j...  4.03 us
    dot_general x1, matrix products, per_device(): jnp.einsum('mcl,pcl->mp', scaled, table, precision=lax.Precision.HIGH, pr...  2.57 us
    dot_general x1, matrix products, per_device(): jnp.einsum('rk,vkd->vrd', perm, proj, preferred_element_type=jnp.float32)  2.17 us

profile of v16, /device:TPU:6, one launch (start us, length us, event | category | flops | bytes accessed | tf_op | source)
XLA Modules:
  0.0 55.8 jit_solution(12720787404318227795)
XLA Ops:
  0.0 0.0 copy-start
  0.0 0.9 %constant_dynamic-slice_fusion.2 = (s32[1,512]{1,0:T(1,128)S(1)}, s32[1,512]{1,0:T(1,128)S(1)}) fusion(s32[8,512]{1,0:T(8,128)} %param.7, s32[]{:T(128)S(6)} %select_n.49, s32[8,512]{1,0:T(8,128)} %param.6), kind=kLoop, calls=%fused_computation.54 | loop fusion | bytes 8196 | tf_op jit(solution)/shard_map/jit(dynamic_index_in_dim)/dynamic_slice | solution.py:221
  0.9 0.2 select_reduce_fusion
  1.1 0.1 iota_add_fusion
  1.2 0.1 reshape.232
  1.4 0.2 reduce_window_sum.11
  1.6 0.1 copy.13
  1.6 0.1 copy.15
  1.7 0.1 convert_reduce_fusion
  1.8 0.1 select_reduce_fusion.1
  1.9 0.1 copy.14
  1.9 0.1 copy.16
  2.1 0.4 fusion.14
  2.5 0.0 copy-done
  2.6 2.2 %fusion.6.proj_ref = bf16[12,512,128]{2,1,0:T(8,128)(2,1)} fusion(bf16[12,512,128]{2,1,0:T(8,128)(2,1)S(1)} %copy-done, s32[512]{0:T(512)S(1)} %bitcast.44), kind=kOutput, calls=%fused_computation.10 | convolution fusion | flops 806354944 | bytes 3147776 | tf_op jit(solution)/shard_map/rk,vkd->vrd/dot_general | solution.py:226
  4.7 6.0 %shard_map.46 = bf16[3,512,1024]{2,1,0:T(8,128)(2,1)} custom-call(bf16[12,512,128]{2,1,0:T(8,128)(2,1)} %fusion.6.proj_ref, bf16[1536,1024]{1,0:T(8,128)(2,1)} %bitcast.39), custom_call_target="tpu_custom_call" | custom-call | tf_op jit(solution)/shard_map/pallas_call | solution.py:202
  10.7 4.0 %bitcast_reduce_fusion = f32[8,8,128,43]{2,3,1,0:T(8,128)} fusion(bf16[3,8,8,8,8,128]{5,3,4,2,1,0:T(8,128)(2,1)} %bitcast.40, bf16[8,8,43,8,8,1]{2,4,3,1,0,5:T(8,128)(2,1)S(1)} %fusion.14), kind=kOutput, calls=%fused_computation | convolution fusion | flops 135970816 | bytes 4907008 | tf_op jit(solution)/shard_map/yzbmc,pyzmcl->pyzbl/dot_general | solution.py:246
  14.8 37.5 %shard_map.47 = f32[43,128]{1,0:T(8,128)} custom-call(f32[8,8,43,128]{3,2,1,0:T(8,128)} %bitcast.41), custom_call_target="tpu_custom_call" | custom-call | tf_op jit(solution)/shard_map/pallas_call | solution.py:172
  52.2 0.9 %fusion.10 = f32[8,8,128]{2,0,1:T(8,128)S(1)} fusion(f32[43,128]{1,0:T(8,128)} %shard_map.47, s32[8,8]{0,1:T(8,128)S(1)} %add_minimum_fusion, f32[8,128]{1,0:T(8,128)S(1)} %get-tuple-element.6, f32[8]{0:T(128)S(1)} %fusion.28), kind=kOutput, calls=%fused_computation.13 | convolution fusion | flops 4278976 | bytes 59168 | tf_op jit(solution)/shard_map/mcj,jl->mcl/dot_general | solution.py:256
  53.2 2.6 %fusion.13 = f32[1,8,1024]{2,1,0:T(8,128)} fusion(f32[8,8,128]{2,0,1:T(8,128)S(1)} %fusion.10, f32[8,128]{1,0:T(8,128)S(1)} %get-tuple-element.5, f32[1024]{0:T(1024)S(1)} %iota_add_fusion.1, f32[8]{0:T(128)S(1)} %fusion.28), kind=kOutput, calls=%fused_computation.16 | convolution fusion | flops 53534720 | bytes 73760 | tf_op jit(solution)/shard_map/mcl,pcl->mp/dot_general | solution.py:269
  (11 shorter events, 0.2 us)
Async XLA Ops:
  0.0 2.5 %copy-start = (bf16[12,512,128]{2,1,0:T(8,128)(2,1)S(1)}, bf16[12,512,128]{2,1,0:T(8,128)(2,1)}, u32[]{:S(2)}) copy-start(bf16[12,512,128]{2,1,0:T(8,128)(2,1)} %param.4) | copy-start | bytes 4718596
